TPU v7x, 512 devices: a whole 4x8x8 slice. The times are simulated.
512 devices in a mesh: cam: 8 (over y_lo, x), sp: 64 (over z, y_hi, core).
Axes of the slice: x: 4, y: 8 (y_hi: 4, y_lo: 2; y = y_hi * 2 + y_lo), z: 8, core: 2. Of those that a mesh axis runs over, the one named last changes fastest.
Arguments:
- q_self: bfloat16 [8, 2048, 2048], P('cam', 'sp'), may hold values from -8 to 8
- keys: bfloat16 [8, 2048, 2048], P('cam', 'sp'), may hold values from -4 to 4
- values: bfloat16 [8, 2048, 2048], P('cam', 'sp'), may hold values from -4 to 4
- q_cross: bfloat16 [8, 2048, 2048], P('cam', 'sp'), may hold values from -8 to 8
- timestep: int32 [1], replicated, may hold values from 0 to 49
- mod_table: float32 [50, 2, 2048], replicated, may hold values from 0.5 to 3
Outputs:
- block_out: bfloat16 [8, 2048, 2048], P('cam', 'sp')
All inputs are finite; a program needn't handle non-finite values.
Results may differ from a plain program's by a relative error of at most 0.0042.
Values may be sent and summed in bfloat16 or wider, within the bound.
No kernel may reach another device: no remote copies, remote signals or barrier semaphores. Data moves between devices by JAX's collectives and lax.ppermute only.
A program may use at most 64 MiB of HBM per device.

v0:
```python
import math

import jax
import jax.numpy as jnp
from jax import lax
from jax.sharding import PartitionSpec as P

HEADS = 16


def passed_along(value, axis, steps):
    count = lax.axis_size(axis)
    pairs = [(source, (source + steps) % count) for source in range(count)]
    return lax.ppermute(value, axis, pairs)


def pick_block(extent, ceiling):
    block_size = min(ceiling, extent)
    while extent % block_size:
        block_size = block_size - 1
    return block_size


def attend(queries, key_rows, value_rows, score_scale):
    query_count, head_dim = queries.shape
    key_count = key_rows.shape[0]
    query_block = pick_block(query_count, 512)
    key_block = pick_block(key_count, 1024)
    key_blocks = key_rows.reshape(key_count // key_block, key_block, head_dim)
    value_blocks = value_rows.reshape(key_count // key_block, key_block, head_dim)

    def per_query(query_part):

        def absorb(state_now, pair_now):
            numerator, runmax, totals = state_now
            key_part, value_part = pair_now
            scores = (
                jnp.einsum("qd,kd->qk", query_part, key_part, preferred_element_type=jnp.float32)
                * score_scale
            )
            newmax = jnp.maximum(runmax, jnp.max(scores, axis=1))
            factor = jnp.exp(runmax - newmax)
            weights = jnp.exp(scores - newmax[:, None])
            totals = totals * factor + jnp.sum(weights, axis=1)
            numerator = numerator * factor[:, None] + jnp.dot(
                weights.astype(jnp.bfloat16), value_part, preferred_element_type=jnp.float32
            )
            return ((numerator, newmax, totals), None)

        start_state = (
            jnp.zeros((query_block, head_dim), jnp.float32),
            jnp.full((query_block,), -jnp.inf, jnp.float32),
            jnp.zeros((query_block,), jnp.float32),
        )
        final_state, _ = lax.scan(absorb, start_state, (key_blocks, value_blocks))
        return final_state

    numerator, runmax, totals = lax.map(
        per_query, queries.reshape(query_count // query_block, query_block, head_dim)
    )
    return (
        numerator.reshape(query_count, head_dim),
        runmax.reshape(query_count),
        totals.reshape(query_count),
    )


def local(q_self, keys, values, q_cross, timestep, mod_table):
    row_count = q_self.shape[1]
    full_width = q_self.shape[2]
    head_count = HEADS
    head_dim = full_width // head_count
    groups = lax.axis_size("sp")
    copies = groups // head_count
    part_rows = row_count // copies
    score_scale = 1.0 / math.sqrt(head_dim)
    query_heads = q_self[0].reshape(row_count, head_count, head_dim)
    key_heads = keys[0].reshape(row_count, head_count, head_dim)
    value_heads = values[0].reshape(row_count, head_count, head_dim)

    def quartered(tensor):
        return (
            tensor.reshape(copies, part_rows, head_count, head_dim)
            .transpose(2, 0, 1, 3)
            .reshape(groups, part_rows, head_dim)
        )

    spread = jnp.broadcast_to(
        query_heads.transpose(1, 0, 2)[:, None], (head_count, copies, row_count, head_dim)
    )
    queries_here = lax.all_to_all(
        spread.reshape(groups, row_count, head_dim), "sp", split_axis=0, concat_axis=1, tiled=True
    )
    keys_here = lax.all_to_all(quartered(key_heads), "sp", split_axis=0, concat_axis=1, tiled=True)
    values_here = lax.all_to_all(
        quartered(value_heads), "sp", split_axis=0, concat_axis=1, tiled=True
    )
    numerator, runmax, totals = attend(queries_here[0], keys_here[0], values_here[0], score_scale)
    numerator, runmax, totals = (
        lax.all_to_all(
            numerator.reshape(groups, row_count, head_dim),
            "sp",
            split_axis=0,
            concat_axis=0,
            tiled=True,
        ),
        lax.all_to_all(
            runmax.reshape(groups, row_count), "sp", split_axis=0, concat_axis=0, tiled=True
        ),
        lax.all_to_all(
            totals.reshape(groups, row_count), "sp", split_axis=0, concat_axis=0, tiled=True
        ),
    )
    numerator = numerator.reshape(head_count, copies, row_count, head_dim)
    runmax = runmax.reshape(head_count, copies, row_count)
    totals = totals.reshape(head_count, copies, row_count)
    topmax = jnp.max(runmax, axis=1)
    factor = jnp.exp(runmax - topmax[:, None])
    numerator = jnp.sum(numerator * factor[..., None], axis=1)
    totals = jnp.sum(totals * factor, axis=1)
    self_out = (
        (numerator / totals[..., None])
        .astype(jnp.bfloat16)
        .transpose(1, 0, 2)
        .reshape(row_count, full_width)
    )
    left_keys, left_values = passed_along((keys[0], values[0]), "cam", 1)
    right_keys, right_values = passed_along((keys[0], values[0]), "cam", -1)
    near_keys = jnp.concatenate([left_keys, right_keys], axis=0).reshape(
        2 * row_count, head_count, head_dim
    )
    near_values = jnp.concatenate([left_values, right_values], axis=0).reshape(
        2 * row_count, head_count, head_dim
    )
    cross_queries = q_cross[0].reshape(row_count, head_count, head_dim)
    scores = (
        jnp.einsum("qhd,khd->hqk", cross_queries, near_keys, preferred_element_type=jnp.float32)
        * score_scale
    )
    row_peak = jnp.max(scores, axis=2)
    weights = jnp.exp(scores - row_peak[..., None])
    totals = jnp.sum(weights, axis=2)
    numerator = jnp.einsum(
        "hqk,khd->qhd",
        weights.astype(jnp.bfloat16),
        near_values,
        preferred_element_type=jnp.float32,
    )
    cross_out = (numerator / totals.T[:, :, None]).reshape(row_count, full_width)
    selector = (jnp.arange(mod_table.shape[0]) == timestep[0]).astype(jnp.float32)
    gate_rows = jnp.tensordot(selector, mod_table, axes=1, precision=lax.Precision.HIGHEST)
    mixed = gate_rows[0] * self_out.astype(jnp.float32) + gate_rows[1] * cross_out
    return mixed.astype(jnp.bfloat16)[None]


def solution(mesh):
    placed = (
        P("cam", "sp", None),
        P("cam", "sp", None),
        P("cam", "sp", None),
        P("cam", "sp", None),
        P(),
        P(),
    )
    return jax.shard_map(
        local, mesh=mesh, in_specs=placed, out_specs=P("cam", "sp", None), check_vma=False
    )
```

profile of v0, /device:TPU:1, one launch (start us, length us, event | category | flops | bytes accessed | tf_op | source)
XLA Modules:
  0.0 154.9 jit_solution(5644704901470905810)
XLA Ops:
  0.0 1.7 %copy.28 = bf16[16,4,8,128]{3,2,1,0:T(8,128)(2,1)} copy(bf16[16,4,8,128]{3,2,0,1:T(8,128)(2,1)} %bitcast.112) | data formatting | bytes 262144 | tf_op jit(solution)/shard_map/transpose | solution.py:84
  1.7 17.8 %all-to-all-start.1 = ((bf16[64,8,128]{2,1,0:T(8,128)(2,1)}), bf16[64,8,128]{2,1,0:T(8,128)(2,1)S(1)}, u32[]{:S(2)}, u32[]{:S(2)}) async-start(bf16[64,8,128]{2,1,0:T(8,128)(2,1)} %bitcast.15), calls=%async_computation.1 | async-start | bytes 262144 | tf_op jit(solution)/shard_map/all_to_all | solution.py:94
  20.1 12.4 %all-to-all-done.1 = bf16[64,8,128]{2,1,0:T(8,128)(2,1)S(1)} async-done(((bf16[64,8,128]{2,1,0:T(8,128)(2,1)}), bf16[64,8,128]{2,1,0:T(8,128)(2,1)S(1)}, u32[]{:S(2)}, u32[]{:S(2)}) %all-to-all-start.1) | async-done | bytes 131104 | tf_op jit(solution)/shard_map/all_to_all | solution.py:94
  32.5 4.6 %all-to-all-start.2 = ((bf16[64,8,128]{2,1,0:T(8,128)(2,1)}), bf16[64,8,128]{2,1,0:T(8,128)(2,1)S(1)}, u32[]{:S(2)}, u32[]{:S(2)}) async-start(bf16[64,8,128]{2,1,0:T(8,128)(2,1)} %bitcast.19), calls=%async_computation.2 | async-start | bytes 262144 | tf_op jit(solution)/shard_map/all_to_all | solution.py:95
  37.2 13.4 %all-to-all-done.2 = bf16[64,8,128]{2,1,0:T(8,128)(2,1)S(1)} async-done(((bf16[64,8,128]{2,1,0:T(8,128)(2,1)}), bf16[64,8,128]{2,1,0:T(8,128)(2,1)S(1)}, u32[]{:S(2)}, u32[]{:S(2)}) %all-to-all-start.2) | async-done | bytes 131104 | tf_op jit(solution)/shard_map/all_to_all | solution.py:95
  50.6 0.9 broadcast_in_dim.18
  51.5 4.5 %all-to-all-start = ((bf16[64,32,128]{2,1,0:T(8,128)(2,1)}), bf16[64,32,128]{2,1,0:T(8,128)(2,1)S(1)}, u32[]{:S(2)}, u32[]{:S(2)}) async-start(bf16[64,32,128]{2,1,0:T(8,128)(2,1)} %bitcast.11), calls=%async_computation | async-start | bytes 1048576 | tf_op jit(solution)/shard_map/all_to_all | solution.py:91
  56.0 19.6 %all-to-all-done = bf16[64,32,128]{2,1,0:T(8,128)(2,1)S(1)} async-done(((bf16[64,32,128]{2,1,0:T(8,128)(2,1)}), bf16[64,32,128]{2,1,0:T(8,128)(2,1)S(1)}, u32[]{:S(2)}, u32[]{:S(2)}) %all-to-all-start) | async-done | bytes 524320 | tf_op jit(solution)/shard_map/all_to_all | solution.py:91
  75.6 6.8 %while.14 = (s32[]{:T(128)}, f32[4,512,128]{2,1,0:T(8,128)}, f32[4,512]{1,0:T(4,128)S(1)}, f32[4,512]{1,0:T(4,128)S(1)}, bf16[4,512,128]{2,1,0:T(8,128)(2,1)S(1)...) while((s32[]{:T(128)}, f32[4,512,128]{2,1,0:T(8,128)}, ...), condition=%wide.region_3.0_spmd, body=%wide.region_0.3_spmd.sunk | while | flops 135857664 | bytes 3830377 | solution.py:58
  76.2 1.0 fusion.43
  77.9 1.0 fusion.43
  79.6 1.0 fusion.43
  81.3 1.0 fusion.43
  83.0 5.9 %all-to-all-start.4 = ((f32[64,1,32]{2,1,0:T(1,128)}), f32[64,1,32]{2,1,0:T(1,128)S(1)}, u32[]{:S(2)}, u32[]{:S(2)}) async-start(f32[64,1,32]{2,1,0:T(1,128)} %bitcast.23), calls=%async_computation.4 | async-start | bytes 65536 | tf_op jit(solution)/shard_map/all_to_all | solution.py:107
  89.0 11.6 %all-to-all-done.4 = f32[64,1,32]{2,1,0:T(1,128)S(1)} async-done(((f32[64,1,32]{2,1,0:T(1,128)}), f32[64,1,32]{2,1,0:T(1,128)S(1)}, u32[]{:S(2)}, u32[]{:S(2)}) %all-to-all-start.4) | async-done | bytes 8224 | tf_op jit(solution)/shard_map/all_to_all | solution.py:107
  100.6 15.8 %all_to_all.56 = f32[64,1,32]{2,1,0:T(1,128)S(1)} all-to-all(f32[64,1,32]{2,1,0:T(1,128)S(1)} %bitcast.109), channel_id=1, replica_groups=mesh['cam'=8,'sp'=64] {'sp'}, dimensions={0} | all-to-all | bytes 16384 | tf_op jit(solution)/shard_map/all_to_all | solution.py:110
  116.4 4.9 %all-to-all-start.3 = ((f32[64,32,128]{2,1,0:T(8,128)}), f32[64,32,128]{2,1,0:T(8,128)S(1)}, u32[]{:S(2)}, u32[]{:S(2)}) async-start(f32[64,32,128]{2,1,0:T(8,128)} %bitcast.106), calls=%async_computation.3 | async-start | bytes 2097152 | tf_op jit(solution)/shard_map/all_to_all | solution.py:100
  121.3 3.1 %collective-permute-start.2 = (bf16[32,2048]{1,0:T(8,128)(2,1)S(1)}, bf16[32,2048]{1,0:T(8,128)(2,1)S(1)}, u32[]{:S(2)}, u32[]{:S(2)}) collective-permute-start(bf16[32,2048]{1,0:T(8,128)(2,1)S(1)} %bitcast.113), channel_id=1, source_target_pairs={{0,64},{64,128},{128,192},{192,256},{256,320},{320,384},{384,448},... | collective-permute-start | bytes 393224 | tf_op jit(solution)/shard_map/ppermute | solution.py:14
  124.4 4.3 %collective-permute-start.3 = (bf16[32,2048]{1,0:T(8,128)(2,1)S(1)}, bf16[32,2048]{1,0:T(8,128)(2,1)S(1)}, u32[]{:S(2)}, u32[]{:S(2)}) collective-permute-start(bf16[32,2048]{1,0:T(8,128)(2,1)S(1)} %bitcast.114), channel_id=1, source_target_pairs={{0,448},{64,0},{128,64},{192,128},{256,192},{320,256},{384,320},{4... | collective-permute-start | bytes 393224 | tf_op jit(solution)/shard_map/ppermute | solution.py:14
  128.7 1.9 %collective-permute-start = (bf16[32,2048]{1,0:T(8,128)(2,1)S(1)}, bf16[32,2048]{1,0:T(8,128)(2,1)S(1)}, u32[]{:S(2)}, u32[]{:S(2)}) collective-permute-start(bf16[32,2048]{1,0:T(8,128)(2,1)S(1)} %bitcast.116), channel_id=1, source_target_pairs={{0,64},{64,128},{128,192},{192,256},{256,320},{320,384},{384,448},... | collective-permute-start | bytes 393224 | tf_op jit(solution)/shard_map/ppermute | solution.py:14
  130.7 5.5 %collective-permute-start.1 = (bf16[32,2048]{1,0:T(8,128)(2,1)S(1)}, bf16[32,2048]{1,0:T(8,128)(2,1)S(1)}, u32[]{:S(2)}, u32[]{:S(2)}) collective-permute-start(bf16[32,2048]{1,0:T(8,128)(2,1)S(1)} %bitcast.117), channel_id=1, source_target_pairs={{0,448},{64,0},{128,64},{192,128},{256,192},{320,256},{384,320},{4... | collective-permute-start | bytes 393224 | tf_op jit(solution)/shard_map/ppermute | solution.py:14
  136.8 0.9 fusion.13
  137.8 12.3 %collective-permute-done.2 = bf16[32,2048]{1,0:T(8,128)(2,1)S(1)} collective-permute-done((bf16[32,2048]{1,0:T(8,128)(2,1)S(1)}, bf16[32,2048]{1,0:T(8,128)(2,1)S(1)}, u32[]{:S(2)}, u32[]{:S(2)}) %collective-permute-start.2) | collective-permute-done | bytes 131104 | tf_op jit(solution)/shard_map/ppermute | solution.py:14
  150.7 2.2 %collective-permute-done = bf16[32,2048]{1,0:T(8,128)(2,1)S(1)} collective-permute-done((bf16[32,2048]{1,0:T(8,128)(2,1)S(1)}, bf16[32,2048]{1,0:T(8,128)(2,1)S(1)}, u32[]{:S(2)}, u32[]{:S(2)}) %collective-permute-start) | collective-permute-done | bytes 131104 | tf_op jit(solution)/shard_map/ppermute | solution.py:14
  (59 shorter events, 6.5 us)
Async XLA Ops:
  0.0 136.8 %copy-start = (f32[50,2,2048]{2,1,0:T(2,128)S(1)}, f32[50,2,2048]{2,1,0:T(2,128)}, u32[]{:S(2)}) copy-start(f32[50,2,2048]{2,1,0:T(2,128)} %param.13) | copy-start | bytes 2457604
  1.7 17.8 %copy-start.4 = (bf16[1,32,2048]{2,1,0:T(8,128)(2,1)S(1)}, bf16[1,32,2048]{2,1,0:T(8,128)(2,1)}, u32[]{:S(2)}) copy-start(bf16[1,32,2048]{2,1,0:T(8,128)(2,1)} %param.10) | copy-start | bytes 393220
  1.7 30.9 %all-to-all-start.1 = ((bf16[64,8,128]{2,1,0:T(8,128)(2,1)}), bf16[64,8,128]{2,1,0:T(8,128)(2,1)S(1)}, u32[]{:S(2)}, u32[]{:S(2)}) async-start(bf16[64,8,128]{2,1,0:T(8,128)(2,1)} %bitcast.15), calls=%async_computation.1 | async-start | bytes 262144 | tf_op jit(solution)/shard_map/all_to_all | solution.py:94
  32.5 4.6 %copy-start.1 = (bf16[1,32,2048]{2,1,0:T(8,128)(2,1)S(1)}, bf16[1,32,2048]{2,1,0:T(8,128)(2,1)}, u32[]{:S(2)}) copy-start(bf16[1,32,2048]{2,1,0:T(8,128)(2,1)} %param.8) | copy-start | bytes 393220
  32.5 18.0 %all-to-all-start.2 = ((bf16[64,8,128]{2,1,0:T(8,128)(2,1)}), bf16[64,8,128]{2,1,0:T(8,128)(2,1)S(1)}, u32[]{:S(2)}, u32[]{:S(2)}) async-start(bf16[64,8,128]{2,1,0:T(8,128)(2,1)} %bitcast.19), calls=%async_computation.2 | async-start | bytes 262144 | tf_op jit(solution)/shard_map/all_to_all | solution.py:95
  51.5 24.1 %all-to-all-start = ((bf16[64,32,128]{2,1,0:T(8,128)(2,1)}), bf16[64,32,128]{2,1,0:T(8,128)(2,1)S(1)}, u32[]{:S(2)}, u32[]{:S(2)}) async-start(bf16[64,32,128]{2,1,0:T(8,128)(2,1)} %bitcast.11), calls=%async_computation | async-start | bytes 1048576 | tf_op jit(solution)/shard_map/all_to_all | solution.py:91
  83.0 17.6 %all-to-all-start.4 = ((f32[64,1,32]{2,1,0:T(1,128)}), f32[64,1,32]{2,1,0:T(1,128)S(1)}, u32[]{:S(2)}, u32[]{:S(2)}) async-start(f32[64,1,32]{2,1,0:T(1,128)} %bitcast.23), calls=%async_computation.4 | async-start | bytes 65536 | tf_op jit(solution)/shard_map/all_to_all | solution.py:107
  116.4 4.9 %copy-start.3 = (bf16[1,32,2048]{2,1,0:T(8,128)(2,1)S(1)}, bf16[1,32,2048]{2,1,0:T(8,128)(2,1)}, u32[]{:S(2)}) copy-start(bf16[1,32,2048]{2,1,0:T(8,128)(2,1)} %param.9) | copy-start | bytes 393220
  116.4 37.0 %all-to-all-start.3 = ((f32[64,32,128]{2,1,0:T(8,128)}), f32[64,32,128]{2,1,0:T(8,128)S(1)}, u32[]{:S(2)}, u32[]{:S(2)}) async-start(f32[64,32,128]{2,1,0:T(8,128)} %bitcast.106), calls=%async_computation.3 | async-start | bytes 2097152 | tf_op jit(solution)/shard_map/all_to_all | solution.py:100
  121.3 28.8 %collective-permute-start.2 = (bf16[32,2048]{1,0:T(8,128)(2,1)S(1)}, bf16[32,2048]{1,0:T(8,128)(2,1)S(1)}, u32[]{:S(2)}, u32[]{:S(2)}) collective-permute-start(bf16[32,2048]{1,0:T(8,128)(2,1)S(1)} %bitcast.113), channel_id=1, source_target_pairs={{0,64},{64,128},{128,192},{192,256},{256,320},{320,384},{384,448},... | collective-permute-start | bytes 393224 | tf_op jit(solution)/shard_map/ppermute | solution.py:14
  124.4 25.6 %collective-permute-start.3 = (bf16[32,2048]{1,0:T(8,128)(2,1)S(1)}, bf16[32,2048]{1,0:T(8,128)(2,1)S(1)}, u32[]{:S(2)}, u32[]{:S(2)}) collective-permute-start(bf16[32,2048]{1,0:T(8,128)(2,1)S(1)} %bitcast.114), channel_id=1, source_target_pairs={{0,448},{64,0},{128,64},{192,128},{256,192},{320,256},{384,320},{4... | collective-permute-start | bytes 393224 | tf_op jit(solution)/shard_map/ppermute | solution.py:14
  128.7 24.2 %collective-permute-start = (bf16[32,2048]{1,0:T(8,128)(2,1)S(1)}, bf16[32,2048]{1,0:T(8,128)(2,1)S(1)}, u32[]{:S(2)}, u32[]{:S(2)}) collective-permute-start(bf16[32,2048]{1,0:T(8,128)(2,1)S(1)} %bitcast.116), channel_id=1, source_target_pairs={{0,64},{64,128},{128,192},{192,256},{256,320},{320,384},{384,448},... | collective-permute-start | bytes 393224 | tf_op jit(solution)/shard_map/ppermute | solution.py:14
  130.7 22.2 %collective-permute-start.1 = (bf16[32,2048]{1,0:T(8,128)(2,1)S(1)}, bf16[32,2048]{1,0:T(8,128)(2,1)S(1)}, u32[]{:S(2)}, u32[]{:S(2)}) collective-permute-start(bf16[32,2048]{1,0:T(8,128)(2,1)S(1)} %bitcast.117), channel_id=1, source_target_pairs={{0,448},{64,0},{128,64},{192,128},{256,192},{320,256},{384,320},{4... | collective-permute-start | bytes 393224 | tf_op jit(solution)/shard_map/ppermute | solution.py:14
  136.8 0.9 copy-start.2
where the time goes:
time: 156 us; the launch traced here: 155 us
  waiting for transfers between devices  71.6 us (46%)
  starting transfers between devices  52.3 us (34%)
  blocking collectives  15.8 us (10%)
  matrix products  6.9 us (4%)
  local copies, waits for them, and re-layouts  4.86 us (3%)
  other arithmetic  2.36 us (2%)
    all_to_all x1, waiting for transfers between devices, local(): lax.all_to_all(spread.reshape(groups, row_count, head_dim), 'sp', split_a...  19.6 us
    all_to_all x1, starting transfers between devices, local(): lax.all_to_all(quartered(key_heads), 'sp', split_axis=0, concat_axis=1, t...  17.8 us
    all_to_all x1, blocking collectives, local(): lax.all_to_all(totals.reshape(groups, row_count), 'sp', split_axis=0, con...  15.8 us
    ppermute x4, starting transfers between devices, passed_along(): return lax.ppermute(value, axis, pairs)  14.8 us
    ppermute x4, waiting for transfers between devices, passed_along(): return lax.ppermute(value, axis, pairs)  14.5 us
    all_to_all x1, waiting for transfers between devices, local(): lax.all_to_all(quartered(value_heads), 'sp', split_axis=0, concat_axis=1,...  13.4 us
    all_to_all x1, waiting for transfers between devices, local(): lax.all_to_all(quartered(key_heads), 'sp', split_axis=0, concat_axis=1, t...  12.4 us
    all_to_all x1, waiting for transfers between devices, local(): lax.all_to_all(runmax.reshape(groups, row_count), 'sp', split_axis=0, con...  11.6 us
  transfers between devices with their start and end apart: 9, of which 6 were waited for; matrix products, arithmetic and copies ran while one was open for 2% of the time, Pallas kernels for 0%

commit v1 on v0

v1 whole, which is shorter than its diff:
```python
import functools
import math

import jax
import jax.numpy as jnp
from jax import lax
from jax.experimental import pallas as pl
from jax.experimental.pallas import tpu as pltpu
from jax.sharding import Mesh
from jax.sharding import PartitionSpec as P

HEADS = 16
LOG2E = 1.4426950408889634

AXES = ("yo", "x", "z", "yh", "yl", "core")
SHAPE = (2, 4, 8, 2, 2, 2)
CAM = ("yo", "x")
SP = ("z", "yh", "yl", "core")
OWNERS = ("z", "yh", "yl")

VMEM = pl.BlockSpec(memory_space=pltpu.VMEM)


def grant(mebibytes):
    return pltpu.CompilerParams(vmem_limit_bytes=mebibytes << 20)


def pack_kernel(q_ref, k_ref, v_ref, piece_ref, near_ref):
    rows = q_ref.shape[0]
    half = rows // 2
    for head in range(HEADS):
        z, yl = divmod(head, 2)
        lanes = slice(head * 128, (head + 1) * 128)
        key = k_ref[:, lanes]
        value = v_ref[:, lanes]
        near_ref[head, :rows, :] = key
        near_ref[head, rows:, :] = value
        for yh in range(2):
            to = (z * 2 + yh) * 2 + yl
            piece_ref[to, :rows, :] = key
            piece_ref[to, rows : 2 * rows, :] = value
            piece_ref[to, 2 * rows :, :] = q_ref[yh * half : (yh + 1) * half, lanes]


def scores_of(query, key):
    return lax.dot_general(query, key, (((1,), (1,)), ((), ())), preferred_element_type=jnp.float32)


def self_kernel(scale, mine_ref, other_ref, out_ref):
    pieces, depth, dim = mine_ref.shape
    part = depth // 5
    block = 8
    keys = [r[:, : 2 * part, :].reshape(pieces * 2 * part, dim) for r in (mine_ref, other_ref)]
    values = [
        r[:, 2 * part : 4 * part, :].reshape(pieces * 2 * part, dim) for r in (mine_ref, other_ref)
    ]
    for start in range(0, pieces, block):
        query = mine_ref[start : start + block, 4 * part :, :].reshape(block * part, dim)
        scores = [scores_of(query, key) for key in keys]
        peak = functools.reduce(
            jnp.maximum, [jnp.max(s, axis=1, keepdims=True) for s in scores]
        )
        weights = [jnp.exp2((s - peak) * scale) for s in scores]
        total = sum(jnp.sum(w, axis=1, keepdims=True) for w in weights)
        numerator = sum(
            jnp.dot(w.astype(jnp.bfloat16), value, preferred_element_type=jnp.float32)
            for w, value in zip(weights, values)
        )
        out_ref[start : start + block] = (
            (numerator / total).astype(jnp.bfloat16).reshape(block, part, dim)
        )


def cross_kernel(scale, step_ref, q_ref, left_ref, right_ref, gate_ref, out_ref):
    rows = q_ref.shape[0]
    for head in range(HEADS):
        lanes = slice(head * 128, (head + 1) * 128)
        query = q_ref[:, lanes]
        left = scores_of(query, left_ref[head, :rows, :])
        right = scores_of(query, right_ref[head, :rows, :])
        peak = jnp.maximum(
            jnp.max(left, axis=1, keepdims=True), jnp.max(right, axis=1, keepdims=True)
        )
        left = jnp.exp2((left - peak) * scale)
        right = jnp.exp2((right - peak) * scale)
        total = jnp.sum(left, axis=1, keepdims=True) + jnp.sum(right, axis=1, keepdims=True)
        numerator = jnp.dot(
            left.astype(jnp.bfloat16), left_ref[head, rows:, :], preferred_element_type=jnp.float32
        ) + jnp.dot(
            right.astype(jnp.bfloat16), right_ref[head, rows:, :], preferred_element_type=jnp.float32
        )
        out_ref[:, lanes] = (numerator / total) * gate_ref[0, 1:2, lanes]


def mix_kernel(step_ref, self_ref, cross_ref, gate_ref, out_ref):
    half = self_ref.shape[1]
    for head in range(HEADS):
        z, yl = divmod(head, 2)
        lanes = slice(head * 128, (head + 1) * 128)
        for yh in range(2):
            rows = slice(yh * half, (yh + 1) * half)
            mine = self_ref[(z * 2 + yh) * 2 + yl].astype(jnp.float32)
            out_ref[0, rows, lanes] = (
                mine * gate_ref[0, 0:1, lanes] + cross_ref[rows, lanes]
            ).astype(jnp.bfloat16)


def shift(value, steps):
    pairs = [(source, (source + steps) % 8) for source in range(8)]
    return lax.ppermute(value, CAM, pairs)


def local(q_self, keys, values, q_cross, timestep, mod_table):
    rows, width = q_self.shape[1:]
    dim = width // HEADS
    scale = LOG2E / math.sqrt(dim)
    full = lambda *shape: pl.BlockSpec(shape, lambda i, step: (0,) * len(shape))
    gates = pl.BlockSpec((1, 2, width), lambda i, step: (step[0], 0, 0))

    pieces, near = pl.pallas_call(
        pack_kernel,
        out_shape=(
            jax.ShapeDtypeStruct((2 * HEADS, 5 * rows // 2, dim), jnp.bfloat16),
            jax.ShapeDtypeStruct((HEADS, 2 * rows, dim), jnp.bfloat16),
        ),
        in_specs=[VMEM] * 3,
        out_specs=(VMEM, VMEM),
        compiler_params=grant(8),
        name="pack",
    )(q_self[0], keys[0], values[0])

    mine = lax.all_to_all(pieces, OWNERS, split_axis=0, concat_axis=0, tiled=True)
    left = shift(near, 1)
    right = shift(near, -1)
    cross = pl.pallas_call(
        functools.partial(cross_kernel, scale),
        out_shape=jax.ShapeDtypeStruct((rows, width), jnp.float32),
        grid_spec=pltpu.PrefetchScalarGridSpec(
            num_scalar_prefetch=1,
            grid=(1,),
            in_specs=[
                full(rows, width),
                full(*near.shape),
                full(*near.shape),
                gates,
            ],
            out_specs=full(rows, width),
        ),
        cost_estimate=pl.CostEstimate(flops=17_000_000, bytes_accessed=900_000, transcendentals=40_000),
        compiler_params=grant(8),
        name="cross",
    )(timestep, q_cross[0], left, right, mod_table)

    other = lax.ppermute(mine, "core", [(0, 1), (1, 0)])
    part = pl.pallas_call(
        functools.partial(self_kernel, scale),
        out_shape=jax.ShapeDtypeStruct((2 * HEADS, rows // 2, dim), jnp.bfloat16),
        in_specs=[VMEM] * 2,
        out_specs=VMEM,
        compiler_params=grant(24),
        name="self",
    )(mine, other)
    own = lax.all_to_all(part, OWNERS, split_axis=0, concat_axis=0, tiled=True)
    return pl.pallas_call(
        mix_kernel,
        out_shape=jax.ShapeDtypeStruct((1, rows, width), jnp.bfloat16),
        grid_spec=pltpu.PrefetchScalarGridSpec(
            num_scalar_prefetch=1,
            grid=(1,),
            in_specs=[full(*own.shape), full(rows, width), gates],
            out_specs=full(1, rows, width),
        ),
        compiler_params=grant(8),
        name="mix",
    )(timestep, own, cross, mod_table)


def solution(mesh):
    fine = Mesh(mesh.devices.reshape(SHAPE), AXES)
    block = P(CAM, SP, None)
    return jax.shard_map(
        local,
        mesh=fine,
        in_specs=(block, block, block, block, P(), P()),
        out_specs=block,
        check_vma=False,
    )
```

time: 156 us -> 74 us (0.47)
  the two profiles are of different devices: /device:TPU:1 before, /device:TPU:6 now
where the time goes in v1:
time: 74 us; the launch traced here: 73.6 us
  blocking collectives  38.2 us (52%)
  starting transfers between devices  16.6 us (22%)
  waiting for transfers between devices  8.11 us (11%)
  Pallas kernels  7.25 us (10%)
  local copies, waits for them, and re-layouts  2.72 us (4%)
  between operations  0.74 us (1%)
    all_to_all x1, blocking collectives, local(): lax.all_to_all(pieces, OWNERS, split_axis=0, concat_axis=0, tiled=True)  38.2 us
    all_to_all x1, waiting for transfers between devices, local(): own = lax.all_to_all(part, OWNERS, split_axis=0, concat_axis=0, tiled=True)  8.1 us
    ppermute x2, starting transfers between devices, shift(): return lax.ppermute(value, CAM, pairs)  8.08 us
    all_to_all x1, starting transfers between devices, local(): own = lax.all_to_all(part, OWNERS, split_axis=0, concat_axis=0, tiled=True)  6.59 us
    pallas_call x1, Pallas kernels, local(): pl.pallas_call(functools.partial(cross_kernel, scale), out_shape=jax.Shap...  3.61 us
    pallas_call x1, Pallas kernels, local(): pl.pallas_call(functools.partial(self_kernel, scale), out_shape=jax.Shape...  2.82 us
    unnamed x10, local copies, waits for them, and re-layouts  2.72 us
    ppermute x1, starting transfers between devices, local(): other = lax.ppermute(mine, 'core', [(0, 1), (1, 0)])  1.91 us
  transfers between devices with their start and end apart: 4, of which 1 were waited for; matrix products, arithmetic and copies ran while one was open for 0% of the time, Pallas kernels for 9%

profile of v1, /device:TPU:6, one launch (start us, length us, event | category | flops | bytes accessed | tf_op | source)
XLA Modules:
  0.0 73.6 jit_solution(5351242651707977322)
XLA Ops:
  0.0 0.0 copy-start.1
  0.0 0.9 %copy-done.1 = bf16[1,32,2048]{2,1,0:T(8,128)(2,1)S(1)} copy-done((bf16[1,32,2048]{2,1,0:T(8,128)(2,1)S(1)}, bf16[1,32,2048]{2,1,0:T(8,128)(2,1)}, u32[]{:S(2)}) %copy-start.1) | copy-done | bytes 131096
  0.9 0.0 copy-start.2
  0.9 0.9 %copy-done.2 = bf16[1,32,2048]{2,1,0:T(8,128)(2,1)S(1)} copy-done((bf16[1,32,2048]{2,1,0:T(8,128)(2,1)S(1)}, bf16[1,32,2048]{2,1,0:T(8,128)(2,1)}, u32[]{:S(2)}) %copy-start.2) | copy-done | bytes 131096
  1.8 0.0 copy-start.3
  1.8 0.9 %copy-done.3 = bf16[1,32,2048]{2,1,0:T(8,128)(2,1)S(1)} copy-done((bf16[1,32,2048]{2,1,0:T(8,128)(2,1)S(1)}, bf16[1,32,2048]{2,1,0:T(8,128)(2,1)}, u32[]{:S(2)}) %copy-start.3) | copy-done | bytes 131096
  2.7 0.1 pack.1
  2.8 38.2 %all_to_all.10.mine_ref = bf16[32,80,128]{2,1,0:T(8,128)(2,1)S(1)} all-to-all(bf16[32,80,128]{2,1,0:T(8,128)(2,1)S(1)} %get-tuple-element.7), channel_id=1, replica_groups=mesh['yo'=2,'x'=4,'z'=8,'yh'=2,'yl'=2,'core'=2] {'z','yh','yl'}, dimensions={0} | all-to-all | bytes 1310720 | tf_op jit(solution)/shard_map/all_to_all | solution.py:132
  41.0 1.9 %collective-permute-start = (bf16[32,80,128]{2,1,0:T(8,128)(2,1)S(1)}, bf16[32,80,128]{2,1,0:T(8,128)(2,1)S(1)}, u32[]{:S(2)}, u32[]{:S(2)}) collective-permute-start(bf16[32,80,128]{2,1,0:T(8,128)(2,1)S(1)} %all_to_all.10.mine_ref), channel_id=1, source_target_pairs={{0,1},{1,0},{2,3},{3,2},{4,5},{5,4},{6,7},{7,6},{8,9},{9,8},{10,11... | collective-permute-start | bytes 1966088 | tf_op jit(solution)/shard_map/ppermute | solution.py:154
  43.0 0.0 copy-start
  43.0 2.9 %collective-permute-start.2 = (bf16[16,64,128]{2,1,0:T(8,128)(2,1)S(1)}, bf16[16,64,128]{2,1,0:T(8,128)(2,1)S(1)}, u32[]{:S(2)}, u32[]{:S(2)}) collective-permute-start(bf16[16,64,128]{2,1,0:T(8,128)(2,1)S(1)} %get-tuple-element.8), channel_id=1, source_target_pairs={{0,448},{64,0},{128,64},{192,128},{256,192},{320,256},{384,320},{4... | collective-permute-start | bytes 786440 | tf_op jit(solution)/shard_map/ppermute | solution.py:110
  45.8 5.2 %collective-permute-start.1 = (bf16[16,64,128]{2,1,0:T(8,128)(2,1)S(1)}, bf16[16,64,128]{2,1,0:T(8,128)(2,1)S(1)}, u32[]{:S(2)}, u32[]{:S(2)}) collective-permute-start(bf16[16,64,128]{2,1,0:T(8,128)(2,1)S(1)} %get-tuple-element.8), channel_id=1, source_target_pairs={{0,64},{64,128},{128,192},{192,256},{256,320},{320,384},{384,448},... | collective-permute-start | bytes 786440 | tf_op jit(solution)/shard_map/ppermute | solution.py:110
  51.1 0.0 collective-permute-done.other_ref
  51.1 2.8 %self.1 = bf16[32,16,128]{2,1,0:T(8,128)(2,1)} custom-call(bf16[32,80,128]{2,1,0:T(8,128)(2,1)S(1)} %all_to_all.10.mine_ref, bf16[32,80,128]{2,1,0:T(8,128)(2,1)S(1)} %collective-permute-done.other_ref), custom_call_target="tpu_custom_call" | custom-call | tf_op jit(solution)/shard_map/self/pallas_call | solution.py:155
  53.9 0.0 copy-start.4
  53.9 6.6 %all-to-all-start.1 = ((bf16[32,16,128]{2,1,0:T(8,128)(2,1)}), bf16[32,16,128]{2,1,0:T(8,128)(2,1)S(1)}, u32[]{:S(2)}, u32[]{:S(2)}) async-start(bf16[32,16,128]{2,1,0:T(8,128)(2,1)} %self.1), calls=%async_computation.1 | async-start | bytes 262144 | tf_op jit(solution)/shard_map/all_to_all | solution.py:163
  61.2 0.0 collective-permute-done.2.right_ref
  61.2 0.0 collective-permute-done.1.left_ref
  61.2 0.0 copy-done
  61.2 0.0 copy-done.4
  61.2 3.6 %cross.1.cross_ref = f32[32,2048]{1,0:T(8,128)S(1)} custom-call(s32[1]{0:T(128)S(6)} %copy.7.step_ref, bf16[32,2048]{1,0:T(8,128)(2,1)S(1)} %bitcast.7, bf16[16,64,128]{2,1,0:T(8,128)(2,1)S(1)} %collective-permute-done.1.left_ref, bf16[16,64,128]{2,1,0:T(8,128)(2,1)S(1)} %collective-permute-done.2.right_ref, f32[50,2,2048]{2,1,0:T(2,128)S(1)} %copy-done), custom_call_target="tpu_custom_call" | custom-call | flops 17000000 | bytes 900000 | tf_op jit(solution)/shard_map/cross/pallas_call | solution.py:135
  64.8 8.1 %all-to-all-done.1.self_ref = bf16[32,16,128]{2,1,0:T(8,128)(2,1)S(1)} async-done(((bf16[32,16,128]{2,1,0:T(8,128)(2,1)}), bf16[32,16,128]{2,1,0:T(8,128)(2,1)S(1)}, u32[]{:S(2)}, u32[]{:S(2)}) %all-to-all-start.1) | async-done | bytes 131104 | tf_op jit(solution)/shard_map/all_to_all | solution.py:163
  72.9 0.7 mix.1
Async XLA Ops:
  0.0 0.9 %copy-start.1 = (bf16[1,32,2048]{2,1,0:T(8,128)(2,1)S(1)}, bf16[1,32,2048]{2,1,0:T(8,128)(2,1)}, u32[]{:S(2)}) copy-start(bf16[1,32,2048]{2,1,0:T(8,128)(2,1)} %param.6) | copy-start | bytes 393220
  0.9 0.9 %copy-start.2 = (bf16[1,32,2048]{2,1,0:T(8,128)(2,1)S(1)}, bf16[1,32,2048]{2,1,0:T(8,128)(2,1)}, u32[]{:S(2)}) copy-start(bf16[1,32,2048]{2,1,0:T(8,128)(2,1)} %param.7) | copy-start | bytes 393220
  1.8 0.9 %copy-start.3 = (bf16[1,32,2048]{2,1,0:T(8,128)(2,1)S(1)}, bf16[1,32,2048]{2,1,0:T(8,128)(2,1)}, u32[]{:S(2)}) copy-start(bf16[1,32,2048]{2,1,0:T(8,128)(2,1)} %param.8) | copy-start | bytes 393220
  41.0 10.0 %collective-permute-start = (bf16[32,80,128]{2,1,0:T(8,128)(2,1)S(1)}, bf16[32,80,128]{2,1,0:T(8,128)(2,1)S(1)}, u32[]{:S(2)}, u32[]{:S(2)}) collective-permute-start(bf16[32,80,128]{2,1,0:T(8,128)(2,1)S(1)} %all_to_all.10.mine_ref), channel_id=1, source_target_pairs={{0,1},{1,0},{2,3},{3,2},{4,5},{5,4},{6,7},{7,6},{8,9},{9,8},{10,11... | collective-permute-start | bytes 1966088 | tf_op jit(solution)/shard_map/ppermute | solution.py:154
  43.0 18.2 %copy-start = (f32[50,2,2048]{2,1,0:T(2,128)S(1)}, f32[50,2,2048]{2,1,0:T(2,128)}, u32[]{:S(2)}) copy-start(f32[50,2,2048]{2,1,0:T(2,128)} %gate_ref.3) | copy-start | bytes 2457604
  43.0 18.2 %collective-permute-start.2 = (bf16[16,64,128]{2,1,0:T(8,128)(2,1)S(1)}, bf16[16,64,128]{2,1,0:T(8,128)(2,1)S(1)}, u32[]{:S(2)}, u32[]{:S(2)}) collective-permute-start(bf16[16,64,128]{2,1,0:T(8,128)(2,1)S(1)} %get-tuple-element.8), channel_id=1, source_target_pairs={{0,448},{64,0},{128,64},{192,128},{256,192},{320,256},{384,320},{4... | collective-permute-start | bytes 786440 | tf_op jit(solution)/shard_map/ppermute | solution.py:110
  45.8 15.3 %collective-permute-start.1 = (bf16[16,64,128]{2,1,0:T(8,128)(2,1)S(1)}, bf16[16,64,128]{2,1,0:T(8,128)(2,1)S(1)}, u32[]{:S(2)}, u32[]{:S(2)}) collective-permute-start(bf16[16,64,128]{2,1,0:T(8,128)(2,1)S(1)} %get-tuple-element.8), channel_id=1, source_target_pairs={{0,64},{64,128},{128,192},{192,256},{256,320},{320,384},{384,448},... | collective-permute-start | bytes 786440 | tf_op jit(solution)/shard_map/ppermute | solution.py:110
  53.9 7.3 %copy-start.4 = (bf16[1,32,2048]{2,1,0:T(8,128)(2,1)S(1)}, bf16[1,32,2048]{2,1,0:T(8,128)(2,1)}, u32[]{:S(2)}) copy-start(bf16[1,32,2048]{2,1,0:T(8,128)(2,1)} %param.9) | copy-start | bytes 393220
  53.9 19.0 %all-to-all-start.1 = ((bf16[32,16,128]{2,1,0:T(8,128)(2,1)}), bf16[32,16,128]{2,1,0:T(8,128)(2,1)S(1)}, u32[]{:S(2)}, u32[]{:S(2)}) async-start(bf16[32,16,128]{2,1,0:T(8,128)(2,1)} %self.1), calls=%async_computation.1 | async-start | bytes 262144 | tf_op jit(solution)/shard_map/all_to_all | solution.py:163

commit v2 on v1

--- a/solution.py
+++ b/solution.py
@@ -25,37 +25,39 @@
     return pltpu.CompilerParams(vmem_limit_bytes=mebibytes << 20)
 
 
-def pack_kernel(q_ref, k_ref, v_ref, piece_ref, near_ref):
+def pack_kernel(q_hbm, k_hbm, v_hbm, piece_ref, near_ref, q_ref, k_ref, v_ref, sems):
     rows = q_ref.shape[0]
-    half = rows // 2
-    for head in range(HEADS):
-        z, yl = divmod(head, 2)
-        lanes = slice(head * 128, (head + 1) * 128)
-        key = k_ref[:, lanes]
-        value = v_ref[:, lanes]
-        near_ref[head, :rows, :] = key
-        near_ref[head, rows:, :] = value
-        for yh in range(2):
-            to = (z * 2 + yh) * 2 + yl
-            piece_ref[to, :rows, :] = key
-            piece_ref[to, rows : 2 * rows, :] = value
-            piece_ref[to, 2 * rows :, :] = q_ref[yh * half : (yh + 1) * half, lanes]
+    copies = [
+        pltpu.make_async_copy(source, target, sems.at[i])
+        for i, (source, target) in enumerate(((k_hbm, k_ref), (v_hbm, v_ref), (q_hbm, q_ref)))
+    ]
+    for copy in copies:
+        copy.start()
+    for i, (copy, part) in enumerate(zip(copies, (k_ref, v_ref, q_ref))):
+        copy.wait()
+        to = slice(i * rows, (i + 1) * rows)
+        for head in range(HEADS):
+            z, yl = divmod(head, 2)
+            block = part[:, head * 128 : (head + 1) * 128]
+            piece_ref[z * 4 + yl, to, :] = block
+            piece_ref[z * 4 + 2 + yl, to, :] = block
+            if i < 2:
+                near_ref[head, to, :] = block
 
 
 def scores_of(query, key):
     return lax.dot_general(query, key, (((1,), (1,)), ((), ())), preferred_element_type=jnp.float32)
 
 
-def self_kernel(scale, mine_ref, other_ref, out_ref):
-    pieces, depth, dim = mine_ref.shape
-    part = depth // 5
-    block = 8
-    keys = [r[:, : 2 * part, :].reshape(pieces * 2 * part, dim) for r in (mine_ref, other_ref)]
-    values = [
-        r[:, 2 * part : 4 * part, :].reshape(pieces * 2 * part, dim) for r in (mine_ref, other_ref)
-    ]
-    for start in range(0, pieces, block):
-        query = mine_ref[start : start + block, 4 * part :, :].reshape(block * part, dim)
+def self_kernel(scale, yh_ref, mine_ref, other_ref, out_ref):
+    lines, _, across, depth, dim = mine_ref.shape
+    part = depth // 3
+    block = 2
+    keys = [r[..., :part, :].reshape(-1, dim) for r in (mine_ref, other_ref)]
+    values = [r[..., part : 2 * part, :].reshape(-1, dim) for r in (mine_ref, other_ref)]
+    for start in range(0, lines, block):
+        query = mine_ref[start : start + block, yh_ref[0], :, 2 * part :, :]
+        query = query.reshape(block * across * part, dim)
         scores = [scores_of(query, key) for key in keys]
         peak = functools.reduce(
             jnp.maximum, [jnp.max(s, axis=1, keepdims=True) for s in scores]
@@ -66,8 +68,8 @@
             jnp.dot(w.astype(jnp.bfloat16), value, preferred_element_type=jnp.float32)
             for w, value in zip(weights, values)
         )
-        out_ref[start : start + block] = (
-            (numerator / total).astype(jnp.bfloat16).reshape(block, part, dim)
+        out_ref[start * across : (start + block) * across] = (
+            (numerator / total).astype(jnp.bfloat16).reshape(block * across, part, dim)
         )
 
 
@@ -93,16 +95,11 @@
 
 
 def mix_kernel(step_ref, self_ref, cross_ref, gate_ref, out_ref):
-    half = self_ref.shape[1]
     for head in range(HEADS):
-        z, yl = divmod(head, 2)
         lanes = slice(head * 128, (head + 1) * 128)
-        for yh in range(2):
-            rows = slice(yh * half, (yh + 1) * half)
-            mine = self_ref[(z * 2 + yh) * 2 + yl].astype(jnp.float32)
-            out_ref[0, rows, lanes] = (
-                mine * gate_ref[0, 0:1, lanes] + cross_ref[rows, lanes]
-            ).astype(jnp.bfloat16)
+        out_ref[0, :, lanes] = (
+            self_ref[head].astype(jnp.float32) * gate_ref[0, 0:1, lanes] + cross_ref[:, lanes]
+        ).astype(jnp.bfloat16)
 
 
 def shift(value, steps):
@@ -120,14 +117,16 @@
     pieces, near = pl.pallas_call(
         pack_kernel,
         out_shape=(
-            jax.ShapeDtypeStruct((2 * HEADS, 5 * rows // 2, dim), jnp.bfloat16),
+            jax.ShapeDtypeStruct((2 * HEADS, 3 * rows, dim), jnp.bfloat16),
             jax.ShapeDtypeStruct((HEADS, 2 * rows, dim), jnp.bfloat16),
         ),
-        in_specs=[VMEM] * 3,
+        in_specs=[pl.BlockSpec(memory_space=pltpu.HBM)] * 3,
         out_specs=(VMEM, VMEM),
+        scratch_shapes=[pltpu.VMEM((rows, width), jnp.bfloat16)] * 3
+        + [pltpu.SemaphoreType.DMA((3,))],
         compiler_params=grant(8),
         name="pack",
-    )(q_self[0], keys[0], values[0])
+    )(*(pltpu.with_memory_space_constraint(x[0], pltpu.HBM) for x in (q_self, keys, values)))
 
     mine = lax.all_to_all(pieces, OWNERS, split_axis=0, concat_axis=0, tiled=True)
     left = shift(near, 1)
@@ -138,29 +137,31 @@
         grid_spec=pltpu.PrefetchScalarGridSpec(
             num_scalar_prefetch=1,
             grid=(1,),
-            in_specs=[
-                full(rows, width),
-                full(*near.shape),
-                full(*near.shape),
-                gates,
-            ],
+            in_specs=[full(rows, width), full(*near.shape), full(*near.shape), gates],
             out_specs=full(rows, width),
         ),
-        cost_estimate=pl.CostEstimate(flops=17_000_000, bytes_accessed=900_000, transcendentals=40_000),
         compiler_params=grant(8),
         name="cross",
     )(timestep, q_cross[0], left, right, mod_table)
-
-    other = lax.ppermute(mine, "core", [(0, 1), (1, 0)])
+    other = lax.ppermute(mine[:, : 2 * rows], "core", [(0, 1), (1, 0)])
+    whole = lambda *shape: pl.BlockSpec(shape, lambda i, yh: (0,) * len(shape))
     part = pl.pallas_call(
         functools.partial(self_kernel, scale),
-        out_shape=jax.ShapeDtypeStruct((2 * HEADS, rows // 2, dim), jnp.bfloat16),
-        in_specs=[VMEM] * 2,
-        out_specs=VMEM,
+        out_shape=jax.ShapeDtypeStruct((HEADS, rows, dim), jnp.bfloat16),
+        grid_spec=pltpu.PrefetchScalarGridSpec(
+            num_scalar_prefetch=1,
+            grid=(1,),
+            in_specs=[whole(8, 2, 2, 3 * rows, dim), whole(8, 2, 2, 2 * rows, dim)],
+            out_specs=whole(HEADS, rows, dim),
+        ),
         compiler_params=grant(24),
         name="self",
-    )(mine, other)
-    own = lax.all_to_all(part, OWNERS, split_axis=0, concat_axis=0, tiled=True)
+    )(
+        lax.axis_index("yh")[None],
+        mine.reshape(8, 2, 2, 3 * rows, dim),
+        other.reshape(8, 2, 2, 2 * rows, dim),
+    )
+    own = lax.all_to_all(part, ("z", "yl"), split_axis=0, concat_axis=0, tiled=True)
     return pl.pallas_call(
         mix_kernel,
         out_shape=jax.ShapeDtypeStruct((1, rows, width), jnp.bfloat16),

time: 74 us -> 71.8 us (0.970)
  the two profiles are of different devices: /device:TPU:6 before, /device:TPU:1 now
where the time goes in v2:
time: 71.8 us; the launch traced here: 71.5 us
  blocking collectives  40.2 us (56%)
  starting transfers between devices  16.8 us (23%)
  Pallas kernels  8.22 us (11%)
  waiting for transfers between devices  5.52 us (8%)
  between operations  0.76 us (1%)
    all_to_all x1, blocking collectives, local(): lax.all_to_all(pieces, OWNERS, split_axis=0, concat_axis=0, tiled=True)  40.2 us
    ppermute x2, starting transfers between devices, shift(): return lax.ppermute(value, CAM, pairs)  7.39 us
    all_to_all x1, waiting for transfers between devices, local(): lax.all_to_all(part, ('z', 'yl'), split_axis=0, concat_axis=0, tiled=True)  5.51 us
    ppermute x1, starting transfers between devices, local(): other = lax.ppermute(mine[:, :2 * rows], 'core', [(0, 1), (1, 0)])  4.89 us
    all_to_all x1, starting transfers between devices, local(): lax.all_to_all(part, ('z', 'yl'), split_axis=0, concat_axis=0, tiled=True)  4.51 us
    pallas_call x1, Pallas kernels, local(): pl.pallas_call(functools.partial(cross_kernel, scale), out_shape=jax.Shap...  3.61 us
    pallas_call x1, Pallas kernels, local(): pl.pallas_call(functools.partial(self_kernel, scale), out_shape=jax.Shape...  2.83 us
  transfers between devices with their start and end apart: 4, of which 1 were waited for; matrix products, arithmetic and copies ran while one was open for 0% of the time, Pallas kernels for 9%

profile of v2, /device:TPU:1, one launch (start us, length us, event | category | flops | bytes accessed | tf_op | source)
XLA Modules:
  0.0 71.5 jit_solution(1833620647381188545)
XLA Ops:
  0.0 1.1 %pack.1 = (bf16[32,96,128]{2,1,0:T(8,128)(2,1)S(1)}, bf16[16,64,128]{2,1,0:T(8,128)(2,1)S(1)}) custom-call(bf16[32,2048]{1,0:T(8,128)(2,1)} %bitcast.10, bf16[32,2048]{1,0:T(8,128)(2,1)} %bitcast.11, bf16[32,2048]{1,0:T(8,128)(2,1)} %bitcast.12), custom_call_target="tpu_custom_call" | custom-call | tf_op jit(solution)/shard_map/pack/pallas_call | solution.py:117
  1.1 40.2 %all_to_all.10 = bf16[32,96,128]{2,1,0:T(8,128)(2,1)S(1)} all-to-all(bf16[32,96,128]{2,1,0:T(8,128)(2,1)S(1)} %get-tuple-element.7), channel_id=1, replica_groups=mesh['yo'=2,'x'=4,'z'=8,'yh'=2,'yl'=2,'core'=2] {'z','yh','yl'}, dimensions={0} | all-to-all | bytes 1572864 | tf_op jit(solution)/shard_map/all_to_all | solution.py:131
  41.3 0.1 slice.4
  41.3 4.9 %collective-permute-start = (bf16[32,64,128]{2,1,0:T(8,128)(2,1)S(1)}, bf16[32,64,128]{2,1,0:T(8,128)(2,1)S(1)}, u32[]{:S(2)}, u32[]{:S(2)}) collective-permute-start(bf16[32,64,128]{2,1,0:T(8,128)(2,1)S(1)} %slice.4), channel_id=1, source_target_pairs={{0,1},{1,0},{2,3},{3,2},{4,5},{5,4},{6,7},{7,6},{8,9},{9,8},{10,11... | collective-permute-start | bytes 1572872 | tf_op jit(solution)/shard_map/ppermute | solution.py:146
  46.2 3.1 %collective-permute-start.1 = (bf16[16,64,128]{2,1,0:T(8,128)(2,1)S(1)}, bf16[16,64,128]{2,1,0:T(8,128)(2,1)S(1)}, u32[]{:S(2)}, u32[]{:S(2)}) collective-permute-start(bf16[16,64,128]{2,1,0:T(8,128)(2,1)S(1)} %get-tuple-element.8), channel_id=1, source_target_pairs={{0,64},{64,128},{128,192},{192,256},{256,320},{320,384},{384,448},... | collective-permute-start | bytes 786440 | tf_op jit(solution)/shard_map/ppermute | solution.py:107
  49.4 4.3 %collective-permute-start.2 = (bf16[16,64,128]{2,1,0:T(8,128)(2,1)S(1)}, bf16[16,64,128]{2,1,0:T(8,128)(2,1)S(1)}, u32[]{:S(2)}, u32[]{:S(2)}) collective-permute-start(bf16[16,64,128]{2,1,0:T(8,128)(2,1)S(1)} %get-tuple-element.8), channel_id=1, source_target_pairs={{0,448},{64,0},{128,64},{192,128},{256,192},{320,256},{384,320},{4... | collective-permute-start | bytes 786440 | tf_op jit(solution)/shard_map/ppermute | solution.py:107
  53.6 0.0 collective-permute-done
  53.6 0.0 copy-start
  53.7 2.8 %self.1 = bf16[16,32,128]{2,1,0:T(8,128)(2,1)} custom-call(s32[1]{0:T(128)} %bitcast.yh_ref, bf16[8,2,2,96,128]{4,3,2,1,0:T(8,128)(2,1)S(1)} %bitcast.7, bf16[8,2,2,64,128]{4,3,2,1,0:T(8,128)(2,1)S(1)} %bitcast.8), custom_call_target="tpu_custom_call" | custom-call | tf_op jit(solution)/shard_map/self/pallas_call | solution.py:148
  56.5 0.0 copy-start.1
  56.5 4.5 %all-to-all-start.1 = ((bf16[16,32,128]{2,1,0:T(8,128)(2,1)}), bf16[16,32,128]{2,1,0:T(8,128)(2,1)S(1)}, u32[]{:S(2)}, u32[]{:S(2)}) async-start(bf16[16,32,128]{2,1,0:T(8,128)(2,1)} %self.1), calls=%async_computation.1 | async-start | bytes 262144 | tf_op jit(solution)/shard_map/all_to_all | solution.py:164
  61.7 0.0 collective-permute-done.1.left_ref
  61.7 0.0 collective-permute-done.2.right_ref
  61.7 0.0 copy-done
  61.7 0.0 copy-done.1
  61.7 3.6 %cross.1.cross_ref = f32[32,2048]{1,0:T(8,128)S(1)} custom-call(s32[1]{0:T(128)S(6)} %copy.7.step_ref, bf16[32,2048]{1,0:T(8,128)(2,1)S(1)} %bitcast.9, bf16[16,64,128]{2,1,0:T(8,128)(2,1)S(1)} %collective-permute-done.1.left_ref, bf16[16,64,128]{2,1,0:T(8,128)(2,1)S(1)} %collective-permute-done.2.right_ref, f32[50,2,2048]{2,1,0:T(2,128)S(1)} %copy-done), custom_call_target="tpu_custom_call" | custom-call | tf_op jit(solution)/shard_map/cross/pallas_call | solution.py:134
  65.3 5.5 %all-to-all-done.1.self_ref = bf16[16,32,128]{2,1,0:T(8,128)(2,1)S(1)} async-done(((bf16[16,32,128]{2,1,0:T(8,128)(2,1)}), bf16[16,32,128]{2,1,0:T(8,128)(2,1)S(1)}, u32[]{:S(2)}, u32[]{:S(2)}) %all-to-all-start.1) | async-done | bytes 131104 | tf_op jit(solution)/shard_map/all_to_all | solution.py:164
  70.8 0.7 mix.1
Async XLA Ops:
  41.3 12.3 %collective-permute-start = (bf16[32,64,128]{2,1,0:T(8,128)(2,1)S(1)}, bf16[32,64,128]{2,1,0:T(8,128)(2,1)S(1)}, u32[]{:S(2)}, u32[]{:S(2)}) collective-permute-start(bf16[32,64,128]{2,1,0:T(8,128)(2,1)S(1)} %slice.4), channel_id=1, source_target_pairs={{0,1},{1,0},{2,3},{3,2},{4,5},{5,4},{6,7},{7,6},{8,9},{9,8},{10,11... | collective-permute-start | bytes 1572872 | tf_op jit(solution)/shard_map/ppermute | solution.py:146
  46.2 15.4 %collective-permute-start.1 = (bf16[16,64,128]{2,1,0:T(8,128)(2,1)S(1)}, bf16[16,64,128]{2,1,0:T(8,128)(2,1)S(1)}, u32[]{:S(2)}, u32[]{:S(2)}) collective-permute-start(bf16[16,64,128]{2,1,0:T(8,128)(2,1)S(1)} %get-tuple-element.8), channel_id=1, source_target_pairs={{0,64},{64,128},{128,192},{192,256},{256,320},{320,384},{384,448},... | collective-permute-start | bytes 786440 | tf_op jit(solution)/shard_map/ppermute | solution.py:107
  49.4 12.3 %collective-permute-start.2 = (bf16[16,64,128]{2,1,0:T(8,128)(2,1)S(1)}, bf16[16,64,128]{2,1,0:T(8,128)(2,1)S(1)}, u32[]{:S(2)}, u32[]{:S(2)}) collective-permute-start(bf16[16,64,128]{2,1,0:T(8,128)(2,1)S(1)} %get-tuple-element.8), channel_id=1, source_target_pairs={{0,448},{64,0},{128,64},{192,128},{256,192},{320,256},{384,320},{4... | collective-permute-start | bytes 786440 | tf_op jit(solution)/shard_map/ppermute | solution.py:107
  53.6 8.0 %copy-start = (f32[50,2,2048]{2,1,0:T(2,128)S(1)}, f32[50,2,2048]{2,1,0:T(2,128)}, u32[]{:S(2)}) copy-start(f32[50,2,2048]{2,1,0:T(2,128)} %gate_ref.3) | copy-start | bytes 2457604
  56.5 5.2 %copy-start.1 = (bf16[1,32,2048]{2,1,0:T(8,128)(2,1)S(1)}, bf16[1,32,2048]{2,1,0:T(8,128)(2,1)}, u32[]{:S(2)}) copy-start(bf16[1,32,2048]{2,1,0:T(8,128)(2,1)} %param.9) | copy-start | bytes 393220
  56.5 14.3 %all-to-all-start.1 = ((bf16[16,32,128]{2,1,0:T(8,128)(2,1)}), bf16[16,32,128]{2,1,0:T(8,128)(2,1)S(1)}, u32[]{:S(2)}, u32[]{:S(2)}) async-start(bf16[16,32,128]{2,1,0:T(8,128)(2,1)} %self.1), calls=%async_computation.1 | async-start | bytes 262144 | tf_op jit(solution)/shard_map/all_to_all | solution.py:164

commit v3 on v2

--- a/solution.py
+++ b/solution.py
@@ -45,6 +45,12 @@
                 near_ref[head, to, :] = block
 
 
+def pick_kernel(step_ref, table_ref, out_ref, sem):
+    copy = pltpu.make_async_copy(table_ref.at[step_ref[0]], out_ref, sem)
+    copy.start()
+    copy.wait()
+
+
 def scores_of(query, key):
     return lax.dot_general(query, key, (((1,), (1,)), ((), ())), preferred_element_type=jnp.float32)
 
@@ -55,6 +61,7 @@
     block = 2
     keys = [r[..., :part, :].reshape(-1, dim) for r in (mine_ref, other_ref)]
     values = [r[..., part : 2 * part, :].reshape(-1, dim) for r in (mine_ref, other_ref)]
+    values = [jnp.concatenate([value, jnp.ones_like(value)], axis=1) for value in values]
     for start in range(0, lines, block):
         query = mine_ref[start : start + block, yh_ref[0], :, 2 * part :, :]
         query = query.reshape(block * across * part, dim)
@@ -62,43 +69,45 @@
         peak = functools.reduce(
             jnp.maximum, [jnp.max(s, axis=1, keepdims=True) for s in scores]
         )
-        weights = [jnp.exp2((s - peak) * scale) for s in scores]
-        total = sum(jnp.sum(w, axis=1, keepdims=True) for w in weights)
-        numerator = sum(
-            jnp.dot(w.astype(jnp.bfloat16), value, preferred_element_type=jnp.float32)
-            for w, value in zip(weights, values)
+        summed = sum(
+            jnp.dot(
+                jnp.exp2((s - peak) * scale).astype(jnp.bfloat16),
+                value,
+                preferred_element_type=jnp.float32,
+            )
+            for s, value in zip(scores, values)
         )
         out_ref[start * across : (start + block) * across] = (
-            (numerator / total).astype(jnp.bfloat16).reshape(block * across, part, dim)
+            (summed[:, :dim] / summed[:, dim:])
+            .astype(jnp.bfloat16)
+            .reshape(block * across, part, dim)
         )
 
 
-def cross_kernel(scale, step_ref, q_ref, left_ref, right_ref, gate_ref, out_ref):
+def cross_kernel(scale, q_ref, left_ref, right_ref, gate_ref, out_ref):
     rows = q_ref.shape[0]
+    both = lambda head, part: jnp.concatenate([left_ref[head, part], right_ref[head, part]], axis=0)
+    lanes = [slice(head * 128, (head + 1) * 128) for head in range(HEADS)]
+    scores = jnp.concatenate(
+        [scores_of(q_ref[:, lanes[head]], both(head, slice(rows))) for head in range(HEADS)],
+        axis=0,
+    )
+    weights = jnp.exp2((scores - jnp.max(scores, axis=1, keepdims=True)) * scale)
+    inverse = 1.0 / jnp.sum(weights, axis=1, keepdims=True)
+    weights = weights.astype(jnp.bfloat16)
     for head in range(HEADS):
-        lanes = slice(head * 128, (head + 1) * 128)
-        query = q_ref[:, lanes]
-        left = scores_of(query, left_ref[head, :rows, :])
-        right = scores_of(query, right_ref[head, :rows, :])
-        peak = jnp.maximum(
-            jnp.max(left, axis=1, keepdims=True), jnp.max(right, axis=1, keepdims=True)
+        at = slice(head * rows, (head + 1) * rows)
+        numerator = jnp.dot(
+            weights[at], both(head, slice(rows, None)), preferred_element_type=jnp.float32
         )
-        left = jnp.exp2((left - peak) * scale)
-        right = jnp.exp2((right - peak) * scale)
-        total = jnp.sum(left, axis=1, keepdims=True) + jnp.sum(right, axis=1, keepdims=True)
-        numerator = jnp.dot(
-            left.astype(jnp.bfloat16), left_ref[head, rows:, :], preferred_element_type=jnp.float32
-        ) + jnp.dot(
-            right.astype(jnp.bfloat16), right_ref[head, rows:, :], preferred_element_type=jnp.float32
-        )
-        out_ref[:, lanes] = (numerator / total) * gate_ref[0, 1:2, lanes]
+        out_ref[:, lanes[head]] = numerator * (inverse[at] * gate_ref[1:2, lanes[head]])
 
 
-def mix_kernel(step_ref, self_ref, cross_ref, gate_ref, out_ref):
+def mix_kernel(self_ref, cross_ref, gate_ref, out_ref):
     for head in range(HEADS):
         lanes = slice(head * 128, (head + 1) * 128)
         out_ref[0, :, lanes] = (
-            self_ref[head].astype(jnp.float32) * gate_ref[0, 0:1, lanes] + cross_ref[:, lanes]
+            self_ref[head].astype(jnp.float32) * gate_ref[0:1, lanes] + cross_ref[:, lanes]
         ).astype(jnp.bfloat16)
 
 
@@ -111,9 +120,6 @@
     rows, width = q_self.shape[1:]
     dim = width // HEADS
     scale = LOG2E / math.sqrt(dim)
-    full = lambda *shape: pl.BlockSpec(shape, lambda i, step: (0,) * len(shape))
-    gates = pl.BlockSpec((1, 2, width), lambda i, step: (step[0], 0, 0))
-
     pieces, near = pl.pallas_call(
         pack_kernel,
         out_shape=(
@@ -131,18 +137,23 @@
     mine = lax.all_to_all(pieces, OWNERS, split_axis=0, concat_axis=0, tiled=True)
     left = shift(near, 1)
     right = shift(near, -1)
+    gates = pl.pallas_call(
+        pick_kernel,
+        out_shape=jax.ShapeDtypeStruct((2, width), jnp.float32),
+        in_specs=[pl.BlockSpec(memory_space=pltpu.SMEM), pl.BlockSpec(memory_space=pltpu.HBM)],
+        out_specs=VMEM,
+        scratch_shapes=[pltpu.SemaphoreType.DMA],
+        compiler_params=grant(1),
+        name="pick",
+    )(timestep, pltpu.with_memory_space_constraint(mod_table, pltpu.HBM))
     cross = pl.pallas_call(
         functools.partial(cross_kernel, scale),
         out_shape=jax.ShapeDtypeStruct((rows, width), jnp.float32),
-        grid_spec=pltpu.PrefetchScalarGridSpec(
-            num_scalar_prefetch=1,
-            grid=(1,),
-            in_specs=[full(rows, width), full(*near.shape), full(*near.shape), gates],
-            out_specs=full(rows, width),
-        ),
+        in_specs=[VMEM] * 4,
+        out_specs=VMEM,
         compiler_params=grant(8),
         name="cross",
-    )(timestep, q_cross[0], left, right, mod_table)
+    )(q_cross[0], left, right, gates)
     other = lax.ppermute(mine[:, : 2 * rows], "core", [(0, 1), (1, 0)])
     whole = lambda *shape: pl.BlockSpec(shape, lambda i, yh: (0,) * len(shape))
     part = pl.pallas_call(
@@ -165,15 +176,11 @@
     return pl.pallas_call(
         mix_kernel,
         out_shape=jax.ShapeDtypeStruct((1, rows, width), jnp.bfloat16),
-        grid_spec=pltpu.PrefetchScalarGridSpec(
-            num_scalar_prefetch=1,
-            grid=(1,),
-            in_specs=[full(*own.shape), full(rows, width), gates],
-            out_specs=full(1, rows, width),
-        ),
+        in_specs=[VMEM] * 3,
+        out_specs=VMEM,
         compiler_params=grant(8),
         name="mix",
-    )(timestep, own, cross, mod_table)
+    )(own, cross, gates)
 
 
 def solution(mesh):

time: 71.8 us -> 71.3 us (level)
  Pallas kernels: 8.22 us -> 5.4 us
  waiting for transfers between devices: 5.52 us -> 7.81 us
    pallas_call x1, Pallas kernels: 3.61 us -> 0.45 us  [local(): pl.pallas_call(functools.partial(cross_kernel, scale), out_shape=jax.Shap...]
    all_to_all x1, waiting for transfers between devices: 5.51 us -> 7.8 us  [local(): lax.all_to_all(part, ('z', 'yl'), split_axis=0, concat_axis=0, tiled=True)]
    pallas_call x0 -> x1, Pallas kernels: none -> 0.76 us  [local(): pl.pallas_call(pick_kernel, out_shape=jax.ShapeDtypeStruct((2, width), jn...]
  transfers between devices with their start and end apart: 4 -> 4, of which waited for: 1 -> 1; matrix products, arithmetic and copies ran while one was open for 0% -> 0% of each run, Pallas kernels for 9% -> 5%
where the time goes in v3:
time: 71.3 us; the launch traced here: 71 us
  blocking collectives  40.2 us (56%)
  starting transfers between devices  16.7 us (23%)
  waiting for transfers between devices  7.81 us (11%)
  Pallas kernels  5.4 us (8%)
  between operations  0.74 us (1%)
    all_to_all x1, blocking collectives, local(): lax.all_to_all(pieces, OWNERS, split_axis=0, concat_axis=0, tiled=True)  40.2 us
    all_to_all x1, waiting for transfers between devices, local(): lax.all_to_all(part, ('z', 'yl'), split_axis=0, concat_axis=0, tiled=True)  7.8 us
    ppermute x2, starting transfers between devices, shift(): return lax.ppermute(value, CAM, pairs)  7.39 us
    ppermute x1, starting transfers between devices, local(): other = lax.ppermute(mine[:, :2 * rows], 'core', [(0, 1), (1, 0)])  4.89 us
    all_to_all x1, starting transfers between devices, local(): lax.all_to_all(part, ('z', 'yl'), split_axis=0, concat_axis=0, tiled=True)  4.38 us
    pallas_call x1, Pallas kernels, local(): pl.pallas_call(functools.partial(self_kernel, scale), out_shape=jax.Shape...  2.4 us
  transfers between devices with their start and end apart: 4, of which 1 were waited for; matrix products, arithmetic and copies ran while one was open for 0% of the time, Pallas kernels for 5%

profile of v3, /device:TPU:1, one launch (start us, length us, event | category | flops | bytes accessed | tf_op | source)
XLA Modules:
  0.0 71.0 jit_solution(11465425081430677786)
XLA Ops:
  0.0 1.1 %pack.1 = (bf16[32,96,128]{2,1,0:T(8,128)(2,1)S(1)}, bf16[16,64,128]{2,1,0:T(8,128)(2,1)S(1)}) custom-call(bf16[32,2048]{1,0:T(8,128)(2,1)} %bitcast.10, bf16[32,2048]{1,0:T(8,128)(2,1)} %bitcast.11, bf16[32,2048]{1,0:T(8,128)(2,1)} %bitcast.12), custom_call_target="tpu_custom_call" | custom-call | tf_op jit(solution)/shard_map/pack/pallas_call | solution.py:123
  1.1 40.2 %all_to_all.10 = bf16[32,96,128]{2,1,0:T(8,128)(2,1)S(1)} all-to-all(bf16[32,96,128]{2,1,0:T(8,128)(2,1)S(1)} %get-tuple-element.7), channel_id=1, replica_groups=mesh['yo'=2,'x'=4,'z'=8,'yh'=2,'yl'=2,'core'=2] {'z','yh','yl'}, dimensions={0} | all-to-all | bytes 1572864 | tf_op jit(solution)/shard_map/all_to_all | solution.py:137
  41.3 0.1 slice.4
  41.3 4.9 %collective-permute-start = (bf16[32,64,128]{2,1,0:T(8,128)(2,1)S(1)}, bf16[32,64,128]{2,1,0:T(8,128)(2,1)S(1)}, u32[]{:S(2)}, u32[]{:S(2)}) collective-permute-start(bf16[32,64,128]{2,1,0:T(8,128)(2,1)S(1)} %slice.4), channel_id=1, source_target_pairs={{0,1},{1,0},{2,3},{3,2},{4,5},{5,4},{6,7},{7,6},{8,9},{9,8},{10,11... | collective-permute-start | bytes 1572872 | tf_op jit(solution)/shard_map/ppermute | solution.py:157
  46.2 3.1 %collective-permute-start.1 = (bf16[16,64,128]{2,1,0:T(8,128)(2,1)S(1)}, bf16[16,64,128]{2,1,0:T(8,128)(2,1)S(1)}, u32[]{:S(2)}, u32[]{:S(2)}) collective-permute-start(bf16[16,64,128]{2,1,0:T(8,128)(2,1)S(1)} %get-tuple-element.8), channel_id=1, source_target_pairs={{0,64},{64,128},{128,192},{192,256},{256,320},{320,384},{384,448},... | collective-permute-start | bytes 786440 | tf_op jit(solution)/shard_map/ppermute | solution.py:116
  49.4 4.3 %collective-permute-start.2 = (bf16[16,64,128]{2,1,0:T(8,128)(2,1)S(1)}, bf16[16,64,128]{2,1,0:T(8,128)(2,1)S(1)}, u32[]{:S(2)}, u32[]{:S(2)}) collective-permute-start(bf16[16,64,128]{2,1,0:T(8,128)(2,1)S(1)} %get-tuple-element.8), channel_id=1, source_target_pairs={{0,448},{64,0},{128,64},{192,128},{256,192},{320,256},{384,320},{4... | collective-permute-start | bytes 786440 | tf_op jit(solution)/shard_map/ppermute | solution.py:116
  53.6 0.0 collective-permute-done
  53.6 2.4 %self.1 = bf16[16,32,128]{2,1,0:T(8,128)(2,1)} custom-call(s32[1]{0:T(128)} %bitcast.yh_ref, bf16[8,2,2,96,128]{4,3,2,1,0:T(8,128)(2,1)S(1)} %bitcast.7, bf16[8,2,2,64,128]{4,3,2,1,0:T(8,128)(2,1)S(1)} %bitcast.8), custom_call_target="tpu_custom_call" | custom-call | tf_op jit(solution)/shard_map/self/pallas_call | solution.py:159
  56.1 4.4 %all-to-all-start.1 = ((bf16[16,32,128]{2,1,0:T(8,128)(2,1)}), bf16[16,32,128]{2,1,0:T(8,128)(2,1)S(1)}, u32[]{:S(2)}, u32[]{:S(2)}) async-start(bf16[16,32,128]{2,1,0:T(8,128)(2,1)} %self.1), calls=%async_computation.1 | async-start | bytes 262144 | tf_op jit(solution)/shard_map/all_to_all | solution.py:175
  61.1 0.0 copy-start
  61.1 0.8 %pick.1.gate_ref = f32[2,2048]{1,0:T(2,128)S(1)} custom-call(s32[1]{0:T(128)S(6)} %copy.7.step_ref, f32[50,2,2048]{2,1,0:T(2,128)} %table_ref.1), custom_call_target="tpu_custom_call" | custom-call | tf_op jit(solution)/shard_map/pick/pallas_call | solution.py:140
  61.9 0.0 collective-permute-done.1.left_ref
  61.9 0.0 collective-permute-done.2.right_ref
  61.9 0.1 copy-done
  62.0 0.5 cross.1.cross_ref
  62.5 7.8 %all-to-all-done.1.self_ref = bf16[16,32,128]{2,1,0:T(8,128)(2,1)S(1)} async-done(((bf16[16,32,128]{2,1,0:T(8,128)(2,1)}), bf16[16,32,128]{2,1,0:T(8,128)(2,1)S(1)}, u32[]{:S(2)}, u32[]{:S(2)}) %all-to-all-start.1) | async-done | bytes 131104 | tf_op jit(solution)/shard_map/all_to_all | solution.py:175
  70.3 0.7 mix.1
Async XLA Ops:
  41.3 12.3 %collective-permute-start = (bf16[32,64,128]{2,1,0:T(8,128)(2,1)S(1)}, bf16[32,64,128]{2,1,0:T(8,128)(2,1)S(1)}, u32[]{:S(2)}, u32[]{:S(2)}) collective-permute-start(bf16[32,64,128]{2,1,0:T(8,128)(2,1)S(1)} %slice.4), channel_id=1, source_target_pairs={{0,1},{1,0},{2,3},{3,2},{4,5},{5,4},{6,7},{7,6},{8,9},{9,8},{10,11... | collective-permute-start | bytes 1572872 | tf_op jit(solution)/shard_map/ppermute | solution.py:157
  46.2 15.6 %collective-permute-start.1 = (bf16[16,64,128]{2,1,0:T(8,128)(2,1)S(1)}, bf16[16,64,128]{2,1,0:T(8,128)(2,1)S(1)}, u32[]{:S(2)}, u32[]{:S(2)}) collective-permute-start(bf16[16,64,128]{2,1,0:T(8,128)(2,1)S(1)} %get-tuple-element.8), channel_id=1, source_target_pairs={{0,64},{64,128},{128,192},{192,256},{256,320},{320,384},{384,448},... | collective-permute-start | bytes 786440 | tf_op jit(solution)/shard_map/ppermute | solution.py:116
  49.4 12.5 %collective-permute-start.2 = (bf16[16,64,128]{2,1,0:T(8,128)(2,1)S(1)}, bf16[16,64,128]{2,1,0:T(8,128)(2,1)S(1)}, u32[]{:S(2)}, u32[]{:S(2)}) collective-permute-start(bf16[16,64,128]{2,1,0:T(8,128)(2,1)S(1)} %get-tuple-element.8), channel_id=1, source_target_pairs={{0,448},{64,0},{128,64},{192,128},{256,192},{320,256},{384,320},{4... | collective-permute-start | bytes 786440 | tf_op jit(solution)/shard_map/ppermute | solution.py:116
  56.1 14.2 %all-to-all-start.1 = ((bf16[16,32,128]{2,1,0:T(8,128)(2,1)}), bf16[16,32,128]{2,1,0:T(8,128)(2,1)S(1)}, u32[]{:S(2)}, u32[]{:S(2)}) async-start(bf16[16,32,128]{2,1,0:T(8,128)(2,1)} %self.1), calls=%async_computation.1 | async-start | bytes 262144 | tf_op jit(solution)/shard_map/all_to_all | solution.py:175
  61.1 0.9 %copy-start = (bf16[1,32,2048]{2,1,0:T(8,128)(2,1)S(1)}, bf16[1,32,2048]{2,1,0:T(8,128)(2,1)}, u32[]{:S(2)}) copy-start(bf16[1,32,2048]{2,1,0:T(8,128)(2,1)} %param.9) | copy-start | bytes 393220

commit v4 on v3

--- a/solution.py
+++ b/solution.py
@@ -6,17 +6,42 @@
 from jax import lax
 from jax.experimental import pallas as pl
 from jax.experimental.pallas import tpu as pltpu
-from jax.sharding import Mesh
 from jax.sharding import PartitionSpec as P
 
 HEADS = 16
 LOG2E = 1.4426950408889634
 
-AXES = ("yo", "x", "z", "yh", "yl", "core")
-SHAPE = (2, 4, 8, 2, 2, 2)
-CAM = ("yo", "x")
-SP = ("z", "yh", "yl", "core")
-OWNERS = ("z", "yh", "yl")
+IN_Z, IN_YH, IN_YL = (5, 6, 7, 0, 1, 2, 3, 4), 1, 0
+OUT_Z, OUT_YL = (4, 5, 6, 7, 0, 1, 2, 3), 1
+
+
+def place(z, yh, yl, core):
+    return ((z * 2 + yh) * 2 + yl) * 2 + core
+
+
+def owners():
+    return [
+        [
+            place(z, yh ^ IN_YH, yl ^ IN_YL, core)
+            for z in IN_Z
+            for yh in range(2)
+            for yl in range(2)
+        ]
+        for core in range(2)
+    ]
+
+
+def half_owners():
+    return [
+        [place(z, yh, yl ^ OUT_YL, core) for z in OUT_Z for yl in range(2)]
+        for yh in range(2)
+        for core in range(2)
+    ]
+
+
+def seat(z, yl):
+    return OUT_Z.index(z) * 2 + (yl ^ OUT_YL)
+
 
 VMEM = pl.BlockSpec(memory_space=pltpu.VMEM)
 
@@ -38,9 +63,10 @@
         to = slice(i * rows, (i + 1) * rows)
         for head in range(HEADS):
             z, yl = divmod(head, 2)
+            line, side = IN_Z.index(z), yl ^ IN_YL
             block = part[:, head * 128 : (head + 1) * 128]
-            piece_ref[z * 4 + yl, to, :] = block
-            piece_ref[z * 4 + 2 + yl, to, :] = block
+            piece_ref[line * 4 + side, to, :] = block
+            piece_ref[line * 4 + 2 + side, to, :] = block
             if i < 2:
                 near_ref[head, to, :] = block
 
@@ -56,32 +82,35 @@
 
 
 def self_kernel(scale, yh_ref, mine_ref, other_ref, out_ref):
-    lines, _, across, depth, dim = mine_ref.shape
+    depths, _, across, depth, dim = mine_ref.shape
     part = depth // 3
-    block = 2
+    block = 4
     keys = [r[..., :part, :].reshape(-1, dim) for r in (mine_ref, other_ref)]
     values = [r[..., part : 2 * part, :].reshape(-1, dim) for r in (mine_ref, other_ref)]
     values = [jnp.concatenate([value, jnp.ones_like(value)], axis=1) for value in values]
-    for start in range(0, lines, block):
+
+    def scored(start):
         query = mine_ref[start : start + block, yh_ref[0], :, 2 * part :, :]
         query = query.reshape(block * across * part, dim)
-        scores = [scores_of(query, key) for key in keys]
+        return [scores_of(query, key) for key in keys]
+
+    ahead = scored(0)
+    for start in range(0, depths, block):
+        scores = ahead
+        if start + block < depths:
+            ahead = scored(start + block)
         peak = functools.reduce(
             jnp.maximum, [jnp.max(s, axis=1, keepdims=True) for s in scores]
         )
+        weights = [jnp.exp2((s - peak) * scale).astype(jnp.bfloat16) for s in scores]
         summed = sum(
-            jnp.dot(
-                jnp.exp2((s - peak) * scale).astype(jnp.bfloat16),
-                value,
-                preferred_element_type=jnp.float32,
-            )
-            for s, value in zip(scores, values)
+            jnp.dot(weight, value, preferred_element_type=jnp.float32)
+            for weight, value in zip(weights, values)
         )
-        out_ref[start * across : (start + block) * across] = (
-            (summed[:, :dim] / summed[:, dim:])
-            .astype(jnp.bfloat16)
-            .reshape(block * across, part, dim)
-        )
+        mixed = (summed[:, :dim] / summed[:, dim:]).astype(jnp.bfloat16)
+        for i in range(block * across):
+            line, side = divmod(start * across + i, across)
+            out_ref[seat(IN_Z[line], side ^ IN_YL)] = mixed[i * part : (i + 1) * part]
 
 
 def cross_kernel(scale, q_ref, left_ref, right_ref, gate_ref, out_ref):
@@ -105,15 +134,16 @@
 
 def mix_kernel(self_ref, cross_ref, gate_ref, out_ref):
     for head in range(HEADS):
+        z, yl = divmod(head, 2)
         lanes = slice(head * 128, (head + 1) * 128)
         out_ref[0, :, lanes] = (
-            self_ref[head].astype(jnp.float32) * gate_ref[0:1, lanes] + cross_ref[:, lanes]
+            self_ref[seat(z, yl)].astype(jnp.float32) * gate_ref[0:1, lanes] + cross_ref[:, lanes]
         ).astype(jnp.bfloat16)
 
 
 def shift(value, steps):
     pairs = [(source, (source + steps) % 8) for source in range(8)]
-    return lax.ppermute(value, CAM, pairs)
+    return lax.ppermute(value, "cam", pairs)
 
 
 def local(q_self, keys, values, q_cross, timestep, mod_table):
@@ -134,7 +164,9 @@
         name="pack",
     )(*(pltpu.with_memory_space_constraint(x[0], pltpu.HBM) for x in (q_self, keys, values)))
 
-    mine = lax.all_to_all(pieces, OWNERS, split_axis=0, concat_axis=0, tiled=True)
+    mine = lax.all_to_all(
+        pieces, "sp", split_axis=0, concat_axis=0, axis_index_groups=owners(), tiled=True
+    )
     left = shift(near, 1)
     right = shift(near, -1)
     gates = pl.pallas_call(
@@ -154,7 +186,7 @@
         compiler_params=grant(8),
         name="cross",
     )(q_cross[0], left, right, gates)
-    other = lax.ppermute(mine[:, : 2 * rows], "core", [(0, 1), (1, 0)])
+    other = lax.ppermute(mine[:, : 2 * rows], "sp", [(i, i ^ 1) for i in range(64)])
     whole = lambda *shape: pl.BlockSpec(shape, lambda i, yh: (0,) * len(shape))
     part = pl.pallas_call(
         functools.partial(self_kernel, scale),
@@ -168,11 +200,13 @@
         compiler_params=grant(24),
         name="self",
     )(
-        lax.axis_index("yh")[None],
+        ((lax.axis_index("sp") // 4) % 2 ^ IN_YH)[None],
         mine.reshape(8, 2, 2, 3 * rows, dim),
         other.reshape(8, 2, 2, 2 * rows, dim),
     )
-    own = lax.all_to_all(part, ("z", "yl"), split_axis=0, concat_axis=0, tiled=True)
+    own = lax.all_to_all(
+        part, "sp", split_axis=0, concat_axis=0, axis_index_groups=half_owners(), tiled=True
+    )
     return pl.pallas_call(
         mix_kernel,
         out_shape=jax.ShapeDtypeStruct((1, rows, width), jnp.bfloat16),
@@ -184,11 +218,10 @@
 
 
 def solution(mesh):
-    fine = Mesh(mesh.devices.reshape(SHAPE), AXES)
-    block = P(CAM, SP, None)
+    block = P("cam", "sp", None)
     return jax.shard_map(
         local,
-        mesh=fine,
+        mesh=mesh,
         in_specs=(block, block, block, block, P(), P()),
         out_specs=block,
         check_vma=False,

time: 71.3 us -> 65.1 us (0.913)
  waiting for transfers between devices: 7.81 us -> 1.65 us
  blocking collectives: 40.2 us -> 35.8 us
  starting transfers between devices: 16.7 us -> 20.7 us
    all_to_all x1, waiting for transfers between devices: 7.8 us -> 1.65 us  [local(): lax.all_to_all(part, 'sp', split_axis=0, concat_axis=0, axis_index_groups...]
    all_to_all x1, blocking collectives: 40.2 us -> 35.8 us  [local(): lax.all_to_all(pieces, 'sp', split_axis=0, concat_axis=0, axis_index_grou...]
    all_to_all x1, starting transfers between devices: 4.38 us -> 8.46 us  [local(): lax.all_to_all(part, 'sp', split_axis=0, concat_axis=0, axis_index_groups...]
where the time goes in v4:
time: 65.1 us; the launch traced here: 64.2 us
  blocking collectives  35.8 us (55%)
  starting transfers between devices  20.7 us (32%)
  Pallas kernels  5.08 us (8%)
  waiting for transfers between devices  1.65 us (3%)
  between operations  0.76 us (1%)
    all_to_all x1, blocking collectives, local(): lax.all_to_all(pieces, 'sp', split_axis=0, concat_axis=0, axis_index_grou...  35.8 us
    all_to_all x1, starting transfers between devices, local(): lax.all_to_all(part, 'sp', split_axis=0, concat_axis=0, axis_index_groups...  8.46 us
    ppermute x2, starting transfers between devices, shift(): return lax.ppermute(value, 'cam', pairs)  7.77 us
    ppermute x1, starting transfers between devices, local(): lax.ppermute(mine[:, :2 * rows], 'sp', [(i, i ^ 1) for i in range(64)])  4.44 us
    pallas_call x1, Pallas kernels, local(): pl.pallas_call(functools.partial(self_kernel, scale), out_shape=jax.Shape...  2.08 us
    all_to_all x1, waiting for transfers between devices, local(): lax.all_to_all(part, 'sp', split_axis=0, concat_axis=0, axis_index_groups...  1.65 us
  transfers between devices with their start and end apart: 4, of which 1 were waited for; matrix products, arithmetic and copies ran while one was open for 0% of the time, Pallas kernels for 5%

profile of v4, /device:TPU:1, one launch (start us, length us, event | category | flops | bytes accessed | tf_op | source)
XLA Modules:
  0.0 64.2 jit_solution(17271260159356155814)
XLA Ops:
  0.0 1.1 %pack.1 = (bf16[32,96,128]{2,1,0:T(8,128)(2,1)S(1)}, bf16[16,64,128]{2,1,0:T(8,128)(2,1)S(1)}) custom-call(bf16[32,2048]{1,0:T(8,128)(2,1)} %bitcast.10, bf16[32,2048]{1,0:T(8,128)(2,1)} %bitcast.11, bf16[32,2048]{1,0:T(8,128)(2,1)} %bitcast.12), custom_call_target="tpu_custom_call" | custom-call | tf_op jit(solution)/shard_map/pack/pallas_call | solution.py:153
  1.1 35.8 %all_to_all.10 = bf16[32,96,128]{2,1,0:T(8,128)(2,1)S(1)} all-to-all(bf16[32,96,128]{2,1,0:T(8,128)(2,1)S(1)} %get-tuple-element.7), channel_id=1, replica_groups={{44,46,40,42,52,54,48,50,60,62,56,58,4,6,0,2,12,14,8,10,20,22,16,18,28,..., dimensions={0} | all-to-all | bytes 1572864 | tf_op jit(solution)/shard_map/all_to_all | solution.py:167
  36.9 0.1 slice.4
  37.0 4.4 %collective-permute-start = (bf16[32,64,128]{2,1,0:T(8,128)(2,1)S(1)}, bf16[32,64,128]{2,1,0:T(8,128)(2,1)S(1)}, u32[]{:S(2)}, u32[]{:S(2)}) collective-permute-start(bf16[32,64,128]{2,1,0:T(8,128)(2,1)S(1)} %slice.4), channel_id=1, source_target_pairs={{0,1},{1,0},{2,3},{3,2},{4,5},{5,4},{6,7},{7,6},{8,9},{9,8},{10,11... | collective-permute-start | bytes 1572872 | tf_op jit(solution)/shard_map/ppermute | solution.py:189
  41.4 3.1 %collective-permute-start.1 = (bf16[16,64,128]{2,1,0:T(8,128)(2,1)S(1)}, bf16[16,64,128]{2,1,0:T(8,128)(2,1)S(1)}, u32[]{:S(2)}, u32[]{:S(2)}) collective-permute-start(bf16[16,64,128]{2,1,0:T(8,128)(2,1)S(1)} %get-tuple-element.8), channel_id=1, source_target_pairs={{0,64},{64,128},{128,192},{192,256},{256,320},{320,384},{384,448},... | collective-permute-start | bytes 786440 | tf_op jit(solution)/shard_map/ppermute | solution.py:146
  44.5 4.7 %collective-permute-start.2 = (bf16[16,64,128]{2,1,0:T(8,128)(2,1)S(1)}, bf16[16,64,128]{2,1,0:T(8,128)(2,1)S(1)}, u32[]{:S(2)}, u32[]{:S(2)}) collective-permute-start(bf16[16,64,128]{2,1,0:T(8,128)(2,1)S(1)} %get-tuple-element.8), channel_id=1, source_target_pairs={{0,448},{64,0},{128,64},{192,128},{256,192},{320,256},{384,320},{4... | collective-permute-start | bytes 786440 | tf_op jit(solution)/shard_map/ppermute | solution.py:146
  49.2 0.0 collective-permute-done
  49.2 2.1 %self.1 = bf16[16,32,128]{2,1,0:T(8,128)(2,1)} custom-call(s32[1]{0:T(128)} %bitcast.yh_ref, bf16[8,2,2,96,128]{4,3,2,1,0:T(8,128)(2,1)S(1)} %bitcast.7, bf16[8,2,2,64,128]{4,3,2,1,0:T(8,128)(2,1)S(1)} %bitcast.8), custom_call_target="tpu_custom_call" | custom-call | tf_op jit(solution)/shard_map/self/pallas_call | solution.py:191
  51.3 8.5 %all-to-all-start.1 = ((bf16[16,32,128]{2,1,0:T(8,128)(2,1)}), bf16[16,32,128]{2,1,0:T(8,128)(2,1)S(1)}, u32[]{:S(2)}, u32[]{:S(2)}) async-start(bf16[16,32,128]{2,1,0:T(8,128)(2,1)} %self.1), calls=%async_computation.1 | async-start | bytes 262144 | tf_op jit(solution)/shard_map/all_to_all | solution.py:207
  60.4 0.0 copy-start
  60.5 0.8 %pick.1.gate_ref = f32[2,2048]{1,0:T(2,128)S(1)} custom-call(s32[1]{0:T(128)S(6)} %copy.7.step_ref, f32[50,2,2048]{2,1,0:T(2,128)} %table_ref.1), custom_call_target="tpu_custom_call" | custom-call | tf_op jit(solution)/shard_map/pick/pallas_call | solution.py:172
  61.2 0.0 collective-permute-done.1.left_ref
  61.2 0.0 collective-permute-done.2.right_ref
  61.2 0.1 copy-done
  61.4 0.5 cross.1.cross_ref
  61.8 1.6 %all-to-all-done.1.self_ref = bf16[16,32,128]{2,1,0:T(8,128)(2,1)S(1)} async-done(((bf16[16,32,128]{2,1,0:T(8,128)(2,1)}), bf16[16,32,128]{2,1,0:T(8,128)(2,1)S(1)}, u32[]{:S(2)}, u32[]{:S(2)}) %all-to-all-start.1) | async-done | bytes 131104 | tf_op jit(solution)/shard_map/all_to_all | solution.py:207
  63.5 0.7 %mix.1 = bf16[1,32,2048]{2,1,0:T(8,128)(2,1)} custom-call(bf16[16,32,128]{2,1,0:T(8,128)(2,1)S(1)} %all-to-all-done.1.self_ref, f32[32,2048]{1,0:T(8,128)S(1)} %cross.1.cross_ref, f32[2,2048]{1,0:T(2,128)S(1)} %pick.1.gate_ref), custom_call_target="tpu_custom_call" | custom-call | tf_op jit(solution)/shard_map/mix/pallas_call | solution.py:210
Async XLA Ops:
  37.0 12.3 %collective-permute-start = (bf16[32,64,128]{2,1,0:T(8,128)(2,1)S(1)}, bf16[32,64,128]{2,1,0:T(8,128)(2,1)S(1)}, u32[]{:S(2)}, u32[]{:S(2)}) collective-permute-start(bf16[32,64,128]{2,1,0:T(8,128)(2,1)S(1)} %slice.4), channel_id=1, source_target_pairs={{0,1},{1,0},{2,3},{3,2},{4,5},{5,4},{6,7},{7,6},{8,9},{9,8},{10,11... | collective-permute-start | bytes 1572872 | tf_op jit(solution)/shard_map/ppermute | solution.py:189
  41.4 19.8 %collective-permute-start.1 = (bf16[16,64,128]{2,1,0:T(8,128)(2,1)S(1)}, bf16[16,64,128]{2,1,0:T(8,128)(2,1)S(1)}, u32[]{:S(2)}, u32[]{:S(2)}) collective-permute-start(bf16[16,64,128]{2,1,0:T(8,128)(2,1)S(1)} %get-tuple-element.8), channel_id=1, source_target_pairs={{0,64},{64,128},{128,192},{192,256},{256,320},{320,384},{384,448},... | collective-permute-start | bytes 786440 | tf_op jit(solution)/shard_map/ppermute | solution.py:146
  44.5 16.7 %collective-permute-start.2 = (bf16[16,64,128]{2,1,0:T(8,128)(2,1)S(1)}, bf16[16,64,128]{2,1,0:T(8,128)(2,1)S(1)}, u32[]{:S(2)}, u32[]{:S(2)}) collective-permute-start(bf16[16,64,128]{2,1,0:T(8,128)(2,1)S(1)} %get-tuple-element.8), channel_id=1, source_target_pairs={{0,448},{64,0},{128,64},{192,128},{256,192},{320,256},{384,320},{4... | collective-permute-start | bytes 786440 | tf_op jit(solution)/shard_map/ppermute | solution.py:146
  51.3 12.1 %all-to-all-start.1 = ((bf16[16,32,128]{2,1,0:T(8,128)(2,1)}), bf16[16,32,128]{2,1,0:T(8,128)(2,1)S(1)}, u32[]{:S(2)}, u32[]{:S(2)}) async-start(bf16[16,32,128]{2,1,0:T(8,128)(2,1)} %self.1), calls=%async_computation.1 | async-start | bytes 262144 | tf_op jit(solution)/shard_map/all_to_all | solution.py:207
  60.4 0.9 %copy-start = (bf16[1,32,2048]{2,1,0:T(8,128)(2,1)S(1)}, bf16[1,32,2048]{2,1,0:T(8,128)(2,1)}, u32[]{:S(2)}) copy-start(bf16[1,32,2048]{2,1,0:T(8,128)(2,1)} %param.9) | copy-start | bytes 393220

commit v5 on v4

--- a/solution.py
+++ b/solution.py
@@ -11,8 +11,8 @@
 HEADS = 16
 LOG2E = 1.4426950408889634
 
-IN_Z, IN_YH, IN_YL = (5, 6, 7, 0, 1, 2, 3, 4), 1, 0
-OUT_Z, OUT_YL = (4, 5, 6, 7, 0, 1, 2, 3), 1
+IN_Z, IN_YH, IN_YL = (5, 0, 1, 2, 3, 4, 6, 7), 1, 0
+OUT_Z, OUT_YL = (4, 0, 1, 2, 3, 5, 6, 7), 1
 
 
 def place(z, yh, yl, core):
@@ -50,25 +50,36 @@
     return pltpu.CompilerParams(vmem_limit_bytes=mebibytes << 20)
 
 
-def pack_kernel(q_hbm, k_hbm, v_hbm, piece_ref, near_ref, q_ref, k_ref, v_ref, sems):
+def pack_kernel(
+    q_hbm, k_hbm, v_hbm, piece_hbm, near_ref, piece_ref, q_ref, k_ref, v_ref, sems, out_sems
+):
     rows = q_ref.shape[0]
+    parts = (k_ref, v_ref, q_ref)
     copies = [
         pltpu.make_async_copy(source, target, sems.at[i])
-        for i, (source, target) in enumerate(((k_hbm, k_ref), (v_hbm, v_ref), (q_hbm, q_ref)))
+        for i, (source, target) in enumerate(zip((k_hbm, v_hbm, q_hbm), parts))
     ]
     for copy in copies:
         copy.start()
-    for i, (copy, part) in enumerate(zip(copies, (k_ref, v_ref, q_ref))):
+    sent = []
+    for i, (copy, part) in enumerate(zip(copies, parts)):
         copy.wait()
         to = slice(i * rows, (i + 1) * rows)
         for head in range(HEADS):
             z, yl = divmod(head, 2)
             line, side = IN_Z.index(z), yl ^ IN_YL
             block = part[:, head * 128 : (head + 1) * 128]
-            piece_ref[line * 4 + side, to, :] = block
-            piece_ref[line * 4 + 2 + side, to, :] = block
-            if i < 2:
-                near_ref[head, to, :] = block
+            piece_ref[i, line * 4 + side] = block
+            piece_ref[i, line * 4 + 2 + side] = block
+        sent.append(
+            pltpu.make_async_copy(piece_ref.at[i], piece_hbm.at[:, to, :], out_sems.at[i])
+        )
+        sent[-1].start()
+    for i, part in enumerate(parts[:2]):
+        for head in range(HEADS):
+            near_ref[head, i * rows : (i + 1) * rows, :] = part[:, head * 128 : (head + 1) * 128]
+    for copy in sent:
+        copy.wait()
 
 
 def pick_kernel(step_ref, table_ref, out_ref, sem):
@@ -113,7 +124,7 @@
             out_ref[seat(IN_Z[line], side ^ IN_YL)] = mixed[i * part : (i + 1) * part]
 
 
-def cross_kernel(scale, q_ref, left_ref, right_ref, gate_ref, out_ref):
+def mix_kernel(scale, self_ref, q_ref, left_ref, right_ref, gate_ref, out_ref):
     rows = q_ref.shape[0]
     both = lambda head, part: jnp.concatenate([left_ref[head, part], right_ref[head, part]], axis=0)
     lanes = [slice(head * 128, (head + 1) * 128) for head in range(HEADS)]
@@ -125,19 +136,14 @@
     inverse = 1.0 / jnp.sum(weights, axis=1, keepdims=True)
     weights = weights.astype(jnp.bfloat16)
     for head in range(HEADS):
+        z, yl = divmod(head, 2)
         at = slice(head * rows, (head + 1) * rows)
         numerator = jnp.dot(
             weights[at], both(head, slice(rows, None)), preferred_element_type=jnp.float32
         )
-        out_ref[:, lanes[head]] = numerator * (inverse[at] * gate_ref[1:2, lanes[head]])
-
-
-def mix_kernel(self_ref, cross_ref, gate_ref, out_ref):
-    for head in range(HEADS):
-        z, yl = divmod(head, 2)
-        lanes = slice(head * 128, (head + 1) * 128)
-        out_ref[0, :, lanes] = (
-            self_ref[seat(z, yl)].astype(jnp.float32) * gate_ref[0:1, lanes] + cross_ref[:, lanes]
+        cross = numerator * (inverse[at] * gate_ref[1:2, lanes[head]])
+        out_ref[0, :, lanes[head]] = (
+            self_ref[seat(z, yl)].astype(jnp.float32) * gate_ref[0:1, lanes[head]] + cross
         ).astype(jnp.bfloat16)
 
 
@@ -157,9 +163,10 @@
             jax.ShapeDtypeStruct((HEADS, 2 * rows, dim), jnp.bfloat16),
         ),
         in_specs=[pl.BlockSpec(memory_space=pltpu.HBM)] * 3,
-        out_specs=(VMEM, VMEM),
-        scratch_shapes=[pltpu.VMEM((rows, width), jnp.bfloat16)] * 3
-        + [pltpu.SemaphoreType.DMA((3,))],
+        out_specs=(pl.BlockSpec(memory_space=pltpu.HBM), VMEM),
+        scratch_shapes=[pltpu.VMEM((3, 2 * HEADS, rows, dim), jnp.bfloat16)]
+        + [pltpu.VMEM((rows, width), jnp.bfloat16)] * 3
+        + [pltpu.SemaphoreType.DMA((3,)), pltpu.SemaphoreType.DMA((3,))],
         compiler_params=grant(8),
         name="pack",
     )(*(pltpu.with_memory_space_constraint(x[0], pltpu.HBM) for x in (q_self, keys, values)))
@@ -178,14 +185,6 @@
         compiler_params=grant(1),
         name="pick",
     )(timestep, pltpu.with_memory_space_constraint(mod_table, pltpu.HBM))
-    cross = pl.pallas_call(
-        functools.partial(cross_kernel, scale),
-        out_shape=jax.ShapeDtypeStruct((rows, width), jnp.float32),
-        in_specs=[VMEM] * 4,
-        out_specs=VMEM,
-        compiler_params=grant(8),
-        name="cross",
-    )(q_cross[0], left, right, gates)
     other = lax.ppermute(mine[:, : 2 * rows], "sp", [(i, i ^ 1) for i in range(64)])
     whole = lambda *shape: pl.BlockSpec(shape, lambda i, yh: (0,) * len(shape))
     part = pl.pallas_call(
@@ -208,13 +207,13 @@
         part, "sp", split_axis=0, concat_axis=0, axis_index_groups=half_owners(), tiled=True
     )
     return pl.pallas_call(
-        mix_kernel,
+        functools.partial(mix_kernel, scale),
         out_shape=jax.ShapeDtypeStruct((1, rows, width), jnp.bfloat16),
-        in_specs=[VMEM] * 3,
+        in_specs=[VMEM] * 5,
         out_specs=VMEM,
         compiler_params=grant(8),
         name="mix",
-    )(own, cross, gates)
+    )(own, q_cross[0], left, right, gates)
 
 
 def solution(mesh):

time: 65.1 us -> 65.5 us (level)
  starting transfers between devices: 20.7 us -> 19.6 us
  blocking collectives: 35.8 us -> 36.8 us
    ppermute x1, starting transfers between devices: 4.44 us -> 3.19 us  [local(): lax.ppermute(mine[:, :2 * rows], 'sp', [(i, i ^ 1) for i in range(64)])]
    all_to_all x1, blocking collectives: 35.8 us -> 36.8 us  [local(): lax.all_to_all(pieces, 'sp', split_axis=0, concat_axis=0, axis_index_grou...]
  transfers between devices with their start and end apart: 4 -> 4, of which waited for: 1 -> 1; matrix products, arithmetic and copies ran while one was open for 0% -> 0% of each run, Pallas kernels for 5% -> 4%
where the time goes in v5:
time: 65.5 us; the launch traced here: 64.7 us
  blocking collectives  36.8 us (56%)
  starting transfers between devices  19.6 us (30%)
  Pallas kernels  5.15 us (8%)
  waiting for transfers between devices  2.27 us (3%)
  between operations  0.76 us (1%)
    all_to_all x1, blocking collectives, local(): lax.all_to_all(pieces, 'sp', split_axis=0, concat_axis=0, axis_index_grou...  36.8 us
    all_to_all x1, starting transfers between devices, local(): lax.all_to_all(part, 'sp', split_axis=0, concat_axis=0, axis_index_groups...  8.46 us
    ppermute x2, starting transfers between devices, shift(): return lax.ppermute(value, 'cam', pairs)  7.97 us
    ppermute x1, starting transfers between devices, local(): lax.ppermute(mine[:, :2 * rows], 'sp', [(i, i ^ 1) for i in range(64)])  3.19 us
    all_to_all x1, waiting for transfers between devices, local(): lax.all_to_all(part, 'sp', split_axis=0, concat_axis=0, axis_index_groups...  2.27 us
    pallas_call x1, Pallas kernels, local(): pl.pallas_call(functools.partial(self_kernel, scale), out_shape=jax.Shape...  2.08 us
  transfers between devices with their start and end apart: 4, of which 1 were waited for; matrix products, arithmetic and copies ran while one was open for 0% of the time, Pallas kernels for 4%

profile of v5, /device:TPU:1, one launch (start us, length us, event | category | flops | bytes accessed | tf_op | source)
XLA Modules:
  0.0 64.7 jit_solution(16676873065245005391)
XLA Ops:
  0.0 1.2 %pack.1 = (bf16[32,96,128]{2,1,0:T(8,128)(2,1)S(1)}, bf16[16,64,128]{2,1,0:T(8,128)(2,1)S(1)}) custom-call(bf16[32,2048]{1,0:T(8,128)(2,1)} %bitcast.10, bf16[32,2048]{1,0:T(8,128)(2,1)} %bitcast.11, bf16[32,2048]{1,0:T(8,128)(2,1)} %bitcast.12), custom_call_target="tpu_custom_call" | custom-call | tf_op jit(solution)/shard_map/pack/pallas_call | solution.py:159
  1.2 36.8 %all_to_all.10 = bf16[32,96,128]{2,1,0:T(8,128)(2,1)S(1)} all-to-all(bf16[32,96,128]{2,1,0:T(8,128)(2,1)S(1)} %get-tuple-element.7), channel_id=1, replica_groups={{44,46,40,42,4,6,0,2,12,14,8,10,20,22,16,18,28,30,24,26,36,38,32,34,52,..., dimensions={0} | all-to-all | bytes 1572864 | tf_op jit(solution)/shard_map/all_to_all | solution.py:174
  38.0 0.1 slice.4
  38.1 3.2 %collective-permute-start = (bf16[32,64,128]{2,1,0:T(8,128)(2,1)S(1)}, bf16[32,64,128]{2,1,0:T(8,128)(2,1)S(1)}, u32[]{:S(2)}, u32[]{:S(2)}) collective-permute-start(bf16[32,64,128]{2,1,0:T(8,128)(2,1)S(1)} %slice.4), channel_id=1, source_target_pairs={{0,1},{1,0},{2,3},{3,2},{4,5},{5,4},{6,7},{7,6},{8,9},{9,8},{10,11... | collective-permute-start | bytes 1572872 | tf_op jit(solution)/shard_map/ppermute | solution.py:188
  41.3 3.1 %collective-permute-start.1 = (bf16[16,64,128]{2,1,0:T(8,128)(2,1)S(1)}, bf16[16,64,128]{2,1,0:T(8,128)(2,1)S(1)}, u32[]{:S(2)}, u32[]{:S(2)}) collective-permute-start(bf16[16,64,128]{2,1,0:T(8,128)(2,1)S(1)} %get-tuple-element.8), channel_id=1, source_target_pairs={{0,64},{64,128},{128,192},{192,256},{256,320},{320,384},{384,448},... | collective-permute-start | bytes 786440 | tf_op jit(solution)/shard_map/ppermute | solution.py:152
  44.4 4.8 %collective-permute-start.2 = (bf16[16,64,128]{2,1,0:T(8,128)(2,1)S(1)}, bf16[16,64,128]{2,1,0:T(8,128)(2,1)S(1)}, u32[]{:S(2)}, u32[]{:S(2)}) collective-permute-start(bf16[16,64,128]{2,1,0:T(8,128)(2,1)S(1)} %get-tuple-element.8), channel_id=1, source_target_pairs={{0,448},{64,0},{128,64},{192,128},{256,192},{320,256},{384,320},{4... | collective-permute-start | bytes 786440 | tf_op jit(solution)/shard_map/ppermute | solution.py:152
  49.3 0.0 collective-permute-done
  49.3 2.1 %self.1 = bf16[16,32,128]{2,1,0:T(8,128)(2,1)} custom-call(s32[1]{0:T(128)} %bitcast.yh_ref, bf16[8,2,2,96,128]{4,3,2,1,0:T(8,128)(2,1)S(1)} %bitcast.7, bf16[8,2,2,64,128]{4,3,2,1,0:T(8,128)(2,1)S(1)} %bitcast.8), custom_call_target="tpu_custom_call" | custom-call | tf_op jit(solution)/shard_map/self/pallas_call | solution.py:190
  51.4 8.5 %all-to-all-start.1 = ((bf16[16,32,128]{2,1,0:T(8,128)(2,1)}), bf16[16,32,128]{2,1,0:T(8,128)(2,1)S(1)}, u32[]{:S(2)}, u32[]{:S(2)}) async-start(bf16[16,32,128]{2,1,0:T(8,128)(2,1)} %self.1), calls=%async_computation.1 | async-start | bytes 262144 | tf_op jit(solution)/shard_map/all_to_all | solution.py:206
  60.5 0.0 copy-start
  60.5 0.8 %pick.1.gate_ref = f32[2,2048]{1,0:T(2,128)S(1)} custom-call(s32[1]{0:T(128)S(6)} %copy.7.step_ref, f32[50,2,2048]{2,1,0:T(2,128)} %table_ref.1), custom_call_target="tpu_custom_call" | custom-call | tf_op jit(solution)/shard_map/pick/pallas_call | solution.py:179
  61.3 0.0 collective-permute-done.1.left_ref
  61.3 0.0 collective-permute-done.2.right_ref
  61.3 2.3 %all-to-all-done.1.self_ref = bf16[16,32,128]{2,1,0:T(8,128)(2,1)S(1)} async-done(((bf16[16,32,128]{2,1,0:T(8,128)(2,1)}), bf16[16,32,128]{2,1,0:T(8,128)(2,1)S(1)}, u32[]{:S(2)}, u32[]{:S(2)}) %all-to-all-start.1) | async-done | bytes 131104 | tf_op jit(solution)/shard_map/all_to_all | solution.py:206
  63.5 0.0 copy-done
  63.5 1.1 %mix.1 = bf16[1,32,2048]{2,1,0:T(8,128)(2,1)} custom-call(bf16[16,32,128]{2,1,0:T(8,128)(2,1)S(1)} %all-to-all-done.1.self_ref, bf16[32,2048]{1,0:T(8,128)(2,1)S(1)} %bitcast.9, bf16[16,64,128]{2,1,0:T(8,128)(2,1)S(1)} %collective-permute-done.1.left_ref, bf16[16,64,128]{2,1,0:T(8,128)(2,1)S(1)} %collective-permute-done.2.right_ref, f32[2,2048]{1,0:T(2,128)S(1)} %pick.1.gate_ref), custom_call_target="tpu_custom_call" | custom-call | tf_op jit(solution)/shard_map/mix/pallas_call | solution.py:209
Async XLA Ops:
  38.1 11.2 %collective-permute-start = (bf16[32,64,128]{2,1,0:T(8,128)(2,1)S(1)}, bf16[32,64,128]{2,1,0:T(8,128)(2,1)S(1)}, u32[]{:S(2)}, u32[]{:S(2)}) collective-permute-start(bf16[32,64,128]{2,1,0:T(8,128)(2,1)S(1)} %slice.4), channel_id=1, source_target_pairs={{0,1},{1,0},{2,3},{3,2},{4,5},{5,4},{6,7},{7,6},{8,9},{9,8},{10,11... | collective-permute-start | bytes 1572872 | tf_op jit(solution)/shard_map/ppermute | solution.py:188
  41.3 20.0 %collective-permute-start.1 = (bf16[16,64,128]{2,1,0:T(8,128)(2,1)S(1)}, bf16[16,64,128]{2,1,0:T(8,128)(2,1)S(1)}, u32[]{:S(2)}, u32[]{:S(2)}) collective-permute-start(bf16[16,64,128]{2,1,0:T(8,128)(2,1)S(1)} %get-tuple-element.8), channel_id=1, source_target_pairs={{0,64},{64,128},{128,192},{192,256},{256,320},{320,384},{384,448},... | collective-permute-start | bytes 786440 | tf_op jit(solution)/shard_map/ppermute | solution.py:152
  44.4 16.9 %collective-permute-start.2 = (bf16[16,64,128]{2,1,0:T(8,128)(2,1)S(1)}, bf16[16,64,128]{2,1,0:T(8,128)(2,1)S(1)}, u32[]{:S(2)}, u32[]{:S(2)}) collective-permute-start(bf16[16,64,128]{2,1,0:T(8,128)(2,1)S(1)} %get-tuple-element.8), channel_id=1, source_target_pairs={{0,448},{64,0},{128,64},{192,128},{256,192},{320,256},{384,320},{4... | collective-permute-start | bytes 786440 | tf_op jit(solution)/shard_map/ppermute | solution.py:152
  51.4 12.2 %all-to-all-start.1 = ((bf16[16,32,128]{2,1,0:T(8,128)(2,1)}), bf16[16,32,128]{2,1,0:T(8,128)(2,1)S(1)}, u32[]{:S(2)}, u32[]{:S(2)}) async-start(bf16[16,32,128]{2,1,0:T(8,128)(2,1)} %self.1), calls=%async_computation.1 | async-start | bytes 262144 | tf_op jit(solution)/shard_map/all_to_all | solution.py:206
  60.5 3.1 %copy-start = (bf16[1,32,2048]{2,1,0:T(8,128)(2,1)S(1)}, bf16[1,32,2048]{2,1,0:T(8,128)(2,1)}, u32[]{:S(2)}) copy-start(bf16[1,32,2048]{2,1,0:T(8,128)(2,1)} %param.9) | copy-start | bytes 393220

commit v6 on v5

--- a/solution.py
+++ b/solution.py
@@ -33,14 +33,14 @@
 
 def half_owners():
     return [
-        [place(z, yh, yl ^ OUT_YL, core) for z in OUT_Z for yl in range(2)]
+        [place(z, yh, yl ^ OUT_YL ^ yh, core) for z in OUT_Z for yl in range(2)]
         for yh in range(2)
         for core in range(2)
     ]
 
 
-def seat(z, yl):
-    return OUT_Z.index(z) * 2 + (yl ^ OUT_YL)
+def seat(z, yl, flip):
+    return OUT_Z.index(z) * 2 + (1 - flip if yl else flip)
 
 
 VMEM = pl.BlockSpec(memory_space=pltpu.VMEM)
@@ -121,10 +121,10 @@
         mixed = (summed[:, :dim] / summed[:, dim:]).astype(jnp.bfloat16)
         for i in range(block * across):
             line, side = divmod(start * across + i, across)
-            out_ref[seat(IN_Z[line], side ^ IN_YL)] = mixed[i * part : (i + 1) * part]
-
-
-def mix_kernel(scale, self_ref, q_ref, left_ref, right_ref, gate_ref, out_ref):
+            out_ref[seat(IN_Z[line], side ^ IN_YL, yh_ref[0])] = mixed[i * part : (i + 1) * part]
+
+
+def mix_kernel(scale, flip_ref, self_ref, q_ref, left_ref, right_ref, gate_ref, out_ref):
     rows = q_ref.shape[0]
     both = lambda head, part: jnp.concatenate([left_ref[head, part], right_ref[head, part]], axis=0)
     lanes = [slice(head * 128, (head + 1) * 128) for head in range(HEADS)]
@@ -143,7 +143,7 @@
         )
         cross = numerator * (inverse[at] * gate_ref[1:2, lanes[head]])
         out_ref[0, :, lanes[head]] = (
-            self_ref[seat(z, yl)].astype(jnp.float32) * gate_ref[0:1, lanes[head]] + cross
+            self_ref[seat(z, yl, flip_ref[0])].astype(jnp.float32) * gate_ref[0:1, lanes[head]] + cross
         ).astype(jnp.bfloat16)
 
 
@@ -156,6 +156,7 @@
     rows, width = q_self.shape[1:]
     dim = width // HEADS
     scale = LOG2E / math.sqrt(dim)
+    lower = (1 - (lax.axis_index("sp") // 4) % 2)[None]
     pieces, near = pl.pallas_call(
         pack_kernel,
         out_shape=(
@@ -199,7 +200,7 @@
         compiler_params=grant(24),
         name="self",
     )(
-        ((lax.axis_index("sp") // 4) % 2 ^ IN_YH)[None],
+        lower,
         mine.reshape(8, 2, 2, 3 * rows, dim),
         other.reshape(8, 2, 2, 2 * rows, dim),
     )
@@ -209,11 +210,11 @@
     return pl.pallas_call(
         functools.partial(mix_kernel, scale),
         out_shape=jax.ShapeDtypeStruct((1, rows, width), jnp.bfloat16),
-        in_specs=[VMEM] * 5,
+        in_specs=[pl.BlockSpec(memory_space=pltpu.SMEM)] + [VMEM] * 5,
         out_specs=VMEM,
         compiler_params=grant(8),
         name="mix",
-    )(own, q_cross[0], left, right, gates)
+    )(lower, own, q_cross[0], left, right, gates)
 
 
 def solution(mesh):

time: 65.5 us -> 65 us (level)
  no operation moved by 1% of the time
where the time goes in v6:
time: 65 us; the launch traced here: 64.7 us
  blocking collectives  36.8 us (57%)
  starting transfers between devices  19.6 us (30%)
  Pallas kernels  5.15 us (8%)
  waiting for transfers between devices  2.27 us (3%)
  between operations  0.76 us (1%)
    all_to_all x1, blocking collectives, local(): lax.all_to_all(pieces, 'sp', split_axis=0, concat_axis=0, axis_index_grou...  36.8 us
    all_to_all x1, starting transfers between devices, local(): lax.all_to_all(part, 'sp', split_axis=0, concat_axis=0, axis_index_groups...  8.46 us
    ppermute x2, starting transfers between devices, shift(): return lax.ppermute(value, 'cam', pairs)  7.97 us
    ppermute x1, starting transfers between devices, local(): lax.ppermute(mine[:, :2 * rows], 'sp', [(i, i ^ 1) for i in range(64)])  3.19 us
    all_to_all x1, waiting for transfers between devices, local(): lax.all_to_all(part, 'sp', split_axis=0, concat_axis=0, axis_index_groups...  2.27 us
    pallas_call x1, Pallas kernels, local(): pl.pallas_call(functools.partial(self_kernel, scale), out_shape=jax.Shape...  2.09 us
  transfers between devices with their start and end apart: 4, of which 1 were waited for; matrix products, arithmetic and copies ran while one was open for 0% of the time, Pallas kernels for 4%

profile of v6, /device:TPU:1, one launch (start us, length us, event | category | flops | bytes accessed | tf_op | source)
XLA Modules:
  0.0 64.7 jit_solution(1356955653491394588)
XLA Ops:
  0.0 1.2 %pack.1 = (bf16[32,96,128]{2,1,0:T(8,128)(2,1)S(1)}, bf16[16,64,128]{2,1,0:T(8,128)(2,1)S(1)}) custom-call(bf16[32,2048]{1,0:T(8,128)(2,1)} %bitcast.10, bf16[32,2048]{1,0:T(8,128)(2,1)} %bitcast.11, bf16[32,2048]{1,0:T(8,128)(2,1)} %bitcast.12), custom_call_target="tpu_custom_call" | custom-call | tf_op jit(solution)/shard_map/pack/pallas_call | solution.py:160
  1.2 36.8 %all_to_all.10 = bf16[32,96,128]{2,1,0:T(8,128)(2,1)S(1)} all-to-all(bf16[32,96,128]{2,1,0:T(8,128)(2,1)S(1)} %get-tuple-element.7), channel_id=1, replica_groups={{44,46,40,42,4,6,0,2,12,14,8,10,20,22,16,18,28,30,24,26,36,38,32,34,52,..., dimensions={0} | all-to-all | bytes 1572864 | tf_op jit(solution)/shard_map/all_to_all | solution.py:175
  38.0 0.1 slice.4
  38.1 3.2 %collective-permute-start = (bf16[32,64,128]{2,1,0:T(8,128)(2,1)S(1)}, bf16[32,64,128]{2,1,0:T(8,128)(2,1)S(1)}, u32[]{:S(2)}, u32[]{:S(2)}) collective-permute-start(bf16[32,64,128]{2,1,0:T(8,128)(2,1)S(1)} %slice.4), channel_id=1, source_target_pairs={{0,1},{1,0},{2,3},{3,2},{4,5},{5,4},{6,7},{7,6},{8,9},{9,8},{10,11... | collective-permute-start | bytes 1572872 | tf_op jit(solution)/shard_map/ppermute | solution.py:189
  41.3 3.1 %collective-permute-start.1 = (bf16[16,64,128]{2,1,0:T(8,128)(2,1)S(1)}, bf16[16,64,128]{2,1,0:T(8,128)(2,1)S(1)}, u32[]{:S(2)}, u32[]{:S(2)}) collective-permute-start(bf16[16,64,128]{2,1,0:T(8,128)(2,1)S(1)} %get-tuple-element.8), channel_id=1, source_target_pairs={{0,64},{64,128},{128,192},{192,256},{256,320},{320,384},{384,448},... | collective-permute-start | bytes 786440 | tf_op jit(solution)/shard_map/ppermute | solution.py:152
  44.4 4.8 %collective-permute-start.2 = (bf16[16,64,128]{2,1,0:T(8,128)(2,1)S(1)}, bf16[16,64,128]{2,1,0:T(8,128)(2,1)S(1)}, u32[]{:S(2)}, u32[]{:S(2)}) collective-permute-start(bf16[16,64,128]{2,1,0:T(8,128)(2,1)S(1)} %get-tuple-element.8), channel_id=1, source_target_pairs={{0,448},{64,0},{128,64},{192,128},{256,192},{320,256},{384,320},{4... | collective-permute-start | bytes 786440 | tf_op jit(solution)/shard_map/ppermute | solution.py:152
  49.3 0.0 collective-permute-done
  49.3 2.1 %self.1 = bf16[16,32,128]{2,1,0:T(8,128)(2,1)} custom-call(s32[1]{0:T(128)} %bitcast.yh_ref.flip_ref, bf16[8,2,2,96,128]{4,3,2,1,0:T(8,128)(2,1)S(1)} %bitcast.7, bf16[8,2,2,64,128]{4,3,2,1,0:T(8,128)(2,1)S(1)} %bitcast.8), custom_call_target="tpu_custom_call" | custom-call | tf_op jit(solution)/shard_map/self/pallas_call | solution.py:191
  51.4 8.5 %all-to-all-start.1 = ((bf16[16,32,128]{2,1,0:T(8,128)(2,1)}), bf16[16,32,128]{2,1,0:T(8,128)(2,1)S(1)}, u32[]{:S(2)}, u32[]{:S(2)}) async-start(bf16[16,32,128]{2,1,0:T(8,128)(2,1)} %self.1), calls=%async_computation.1 | async-start | bytes 262144 | tf_op jit(solution)/shard_map/all_to_all | solution.py:207
  60.5 0.0 copy-start
  60.5 0.8 %pick.1.gate_ref = f32[2,2048]{1,0:T(2,128)S(1)} custom-call(s32[1]{0:T(128)S(6)} %copy.7.step_ref, f32[50,2,2048]{2,1,0:T(2,128)} %table_ref.1), custom_call_target="tpu_custom_call" | custom-call | tf_op jit(solution)/shard_map/pick/pallas_call | solution.py:180
  61.3 0.0 collective-permute-done.1.left_ref
  61.3 0.0 collective-permute-done.2.right_ref
  61.3 2.3 %all-to-all-done.1.self_ref = bf16[16,32,128]{2,1,0:T(8,128)(2,1)S(1)} async-done(((bf16[16,32,128]{2,1,0:T(8,128)(2,1)}), bf16[16,32,128]{2,1,0:T(8,128)(2,1)S(1)}, u32[]{:S(2)}, u32[]{:S(2)}) %all-to-all-start.1) | async-done | bytes 131104 | tf_op jit(solution)/shard_map/all_to_all | solution.py:207
  63.6 0.0 copy-done
  63.6 1.1 %mix.1 = bf16[1,32,2048]{2,1,0:T(8,128)(2,1)} custom-call(s32[1]{0:T(128)} %bitcast.yh_ref.flip_ref, bf16[16,32,128]{2,1,0:T(8,128)(2,1)S(1)} %all-to-all-done.1.self_ref, bf16[32,2048]{1,0:T(8,128)(2,1)S(1)} %bitcast.9, bf16[16,64,128]{2,1,0:T(8,128)(2,1)S(1)} %collective-permute-done.1.left_ref, bf16[16,64,128]{2,1,0:T(8,128)(2,1)S(1)} %collective-permute-done.2.right_ref, ...), custom_call_target="tpu_custom_call" | custom-call | tf_op jit(solution)/shard_map/mix/pallas_call | solution.py:210
Async XLA Ops:
  38.1 11.2 %collective-permute-start = (bf16[32,64,128]{2,1,0:T(8,128)(2,1)S(1)}, bf16[32,64,128]{2,1,0:T(8,128)(2,1)S(1)}, u32[]{:S(2)}, u32[]{:S(2)}) collective-permute-start(bf16[32,64,128]{2,1,0:T(8,128)(2,1)S(1)} %slice.4), channel_id=1, source_target_pairs={{0,1},{1,0},{2,3},{3,2},{4,5},{5,4},{6,7},{7,6},{8,9},{9,8},{10,11... | collective-permute-start | bytes 1572872 | tf_op jit(solution)/shard_map/ppermute | solution.py:189
  41.3 20.0 %collective-permute-start.1 = (bf16[16,64,128]{2,1,0:T(8,128)(2,1)S(1)}, bf16[16,64,128]{2,1,0:T(8,128)(2,1)S(1)}, u32[]{:S(2)}, u32[]{:S(2)}) collective-permute-start(bf16[16,64,128]{2,1,0:T(8,128)(2,1)S(1)} %get-tuple-element.8), channel_id=1, source_target_pairs={{0,64},{64,128},{128,192},{192,256},{256,320},{320,384},{384,448},... | collective-permute-start | bytes 786440 | tf_op jit(solution)/shard_map/ppermute | solution.py:152
  44.4 16.9 %collective-permute-start.2 = (bf16[16,64,128]{2,1,0:T(8,128)(2,1)S(1)}, bf16[16,64,128]{2,1,0:T(8,128)(2,1)S(1)}, u32[]{:S(2)}, u32[]{:S(2)}) collective-permute-start(bf16[16,64,128]{2,1,0:T(8,128)(2,1)S(1)} %get-tuple-element.8), channel_id=1, source_target_pairs={{0,448},{64,0},{128,64},{192,128},{256,192},{320,256},{384,320},{4... | collective-permute-start | bytes 786440 | tf_op jit(solution)/shard_map/ppermute | solution.py:152
  51.4 12.2 %all-to-all-start.1 = ((bf16[16,32,128]{2,1,0:T(8,128)(2,1)}), bf16[16,32,128]{2,1,0:T(8,128)(2,1)S(1)}, u32[]{:S(2)}, u32[]{:S(2)}) async-start(bf16[16,32,128]{2,1,0:T(8,128)(2,1)} %self.1), calls=%async_computation.1 | async-start | bytes 262144 | tf_op jit(solution)/shard_map/all_to_all | solution.py:207
  60.5 3.1 %copy-start = (bf16[1,32,2048]{2,1,0:T(8,128)(2,1)S(1)}, bf16[1,32,2048]{2,1,0:T(8,128)(2,1)}, u32[]{:S(2)}) copy-start(bf16[1,32,2048]{2,1,0:T(8,128)(2,1)} %param.9) | copy-start | bytes 393220

commit v7 on v6

--- a/solution.py
+++ b/solution.py
@@ -12,7 +12,7 @@
 LOG2E = 1.4426950408889634
 
 IN_Z, IN_YH, IN_YL = (5, 0, 1, 2, 3, 4, 6, 7), 1, 0
-OUT_Z, OUT_YL = (4, 0, 1, 2, 3, 5, 6, 7), 1
+OUT_Z, OUT_YL = ((4, 0, 1, 2, 3, 5, 6, 7), (5, 0, 1, 2, 3, 4, 6, 7)), 1
 
 
 def place(z, yh, yl, core):
@@ -33,14 +33,15 @@
 
 def half_owners():
     return [
-        [place(z, yh, yl ^ OUT_YL ^ yh, core) for z in OUT_Z for yl in range(2)]
+        [place(z, yh, yl ^ OUT_YL ^ yh, core) for z in OUT_Z[yh] for yl in range(2)]
         for yh in range(2)
         for core in range(2)
     ]
 
 
 def seat(z, yl, flip):
-    return OUT_Z.index(z) * 2 + (1 - flip if yl else flip)
+    below, above = (order.index(z) for order in OUT_Z)
+    return (above + (below - above) * flip) * 2 + (1 - flip if yl else flip)
 
 
 VMEM = pl.BlockSpec(memory_space=pltpu.VMEM)

time: 65 us -> 65.2 us (level)
  no operation moved by 1% of the time
where the time goes in v7:
time: 65.2 us; the launch traced here: 64.7 us
  blocking collectives  36.8 us (56%)
  starting transfers between devices  19.6 us (30%)
  Pallas kernels  5.15 us (8%)
  waiting for transfers between devices  2.27 us (3%)
  between operations  0.76 us (1%)
    all_to_all x1, blocking collectives, local(): lax.all_to_all(pieces, 'sp', split_axis=0, concat_axis=0, axis_index_grou...  36.8 us
    all_to_all x1, starting transfers between devices, local(): lax.all_to_all(part, 'sp', split_axis=0, concat_axis=0, axis_index_groups...  8.46 us
    ppermute x2, starting transfers between devices, shift(): return lax.ppermute(value, 'cam', pairs)  7.97 us
    ppermute x1, starting transfers between devices, local(): lax.ppermute(mine[:, :2 * rows], 'sp', [(i, i ^ 1) for i in range(64)])  3.19 us
    all_to_all x1, waiting for transfers between devices, local(): lax.all_to_all(part, 'sp', split_axis=0, concat_axis=0, axis_index_groups...  2.27 us
    pallas_call x1, Pallas kernels, local(): pl.pallas_call(functools.partial(self_kernel, scale), out_shape=jax.Shape...  2.09 us
  transfers between devices with their start and end apart: 4, of which 1 were waited for; matrix products, arithmetic and copies ran while one was open for 0% of the time, Pallas kernels for 4%

profile of v7, /device:TPU:1, one launch (start us, length us, event | category | flops | bytes accessed | tf_op | source)
XLA Modules:
  0.0 64.7 jit_solution(5948324656309892714)
XLA Ops:
  0.0 1.2 %pack.1 = (bf16[32,96,128]{2,1,0:T(8,128)(2,1)S(1)}, bf16[16,64,128]{2,1,0:T(8,128)(2,1)S(1)}) custom-call(bf16[32,2048]{1,0:T(8,128)(2,1)} %bitcast.10, bf16[32,2048]{1,0:T(8,128)(2,1)} %bitcast.11, bf16[32,2048]{1,0:T(8,128)(2,1)} %bitcast.12), custom_call_target="tpu_custom_call" | custom-call | tf_op jit(solution)/shard_map/pack/pallas_call | solution.py:161
  1.2 36.8 %all_to_all.10 = bf16[32,96,128]{2,1,0:T(8,128)(2,1)S(1)} all-to-all(bf16[32,96,128]{2,1,0:T(8,128)(2,1)S(1)} %get-tuple-element.7), channel_id=1, replica_groups={{44,46,40,42,4,6,0,2,12,14,8,10,20,22,16,18,28,30,24,26,36,38,32,34,52,..., dimensions={0} | all-to-all | bytes 1572864 | tf_op jit(solution)/shard_map/all_to_all | solution.py:176
  38.0 0.1 slice.4
  38.1 3.2 %collective-permute-start = (bf16[32,64,128]{2,1,0:T(8,128)(2,1)S(1)}, bf16[32,64,128]{2,1,0:T(8,128)(2,1)S(1)}, u32[]{:S(2)}, u32[]{:S(2)}) collective-permute-start(bf16[32,64,128]{2,1,0:T(8,128)(2,1)S(1)} %slice.4), channel_id=1, source_target_pairs={{0,1},{1,0},{2,3},{3,2},{4,5},{5,4},{6,7},{7,6},{8,9},{9,8},{10,11... | collective-permute-start | bytes 1572872 | tf_op jit(solution)/shard_map/ppermute | solution.py:190
  41.3 3.1 %collective-permute-start.1 = (bf16[16,64,128]{2,1,0:T(8,128)(2,1)S(1)}, bf16[16,64,128]{2,1,0:T(8,128)(2,1)S(1)}, u32[]{:S(2)}, u32[]{:S(2)}) collective-permute-start(bf16[16,64,128]{2,1,0:T(8,128)(2,1)S(1)} %get-tuple-element.8), channel_id=1, source_target_pairs={{0,64},{64,128},{128,192},{192,256},{256,320},{320,384},{384,448},... | collective-permute-start | bytes 786440 | tf_op jit(solution)/shard_map/ppermute | solution.py:153
  44.4 4.8 %collective-permute-start.2 = (bf16[16,64,128]{2,1,0:T(8,128)(2,1)S(1)}, bf16[16,64,128]{2,1,0:T(8,128)(2,1)S(1)}, u32[]{:S(2)}, u32[]{:S(2)}) collective-permute-start(bf16[16,64,128]{2,1,0:T(8,128)(2,1)S(1)} %get-tuple-element.8), channel_id=1, source_target_pairs={{0,448},{64,0},{128,64},{192,128},{256,192},{320,256},{384,320},{4... | collective-permute-start | bytes 786440 | tf_op jit(solution)/shard_map/ppermute | solution.py:153
  49.3 0.0 collective-permute-done
  49.3 2.1 %self.1 = bf16[16,32,128]{2,1,0:T(8,128)(2,1)} custom-call(s32[1]{0:T(128)} %bitcast.yh_ref.flip_ref, bf16[8,2,2,96,128]{4,3,2,1,0:T(8,128)(2,1)S(1)} %bitcast.7, bf16[8,2,2,64,128]{4,3,2,1,0:T(8,128)(2,1)S(1)} %bitcast.8), custom_call_target="tpu_custom_call" | custom-call | tf_op jit(solution)/shard_map/self/pallas_call | solution.py:192
  51.4 8.5 %all-to-all-start.1 = ((bf16[16,32,128]{2,1,0:T(8,128)(2,1)}), bf16[16,32,128]{2,1,0:T(8,128)(2,1)S(1)}, u32[]{:S(2)}, u32[]{:S(2)}) async-start(bf16[16,32,128]{2,1,0:T(8,128)(2,1)} %self.1), calls=%async_computation.1 | async-start | bytes 262144 | tf_op jit(solution)/shard_map/all_to_all | solution.py:208
  60.5 0.0 copy-start
  60.5 0.8 %pick.1.gate_ref = f32[2,2048]{1,0:T(2,128)S(1)} custom-call(s32[1]{0:T(128)S(6)} %copy.7.step_ref, f32[50,2,2048]{2,1,0:T(2,128)} %table_ref.1), custom_call_target="tpu_custom_call" | custom-call | tf_op jit(solution)/shard_map/pick/pallas_call | solution.py:181
  61.3 0.0 collective-permute-done.1.left_ref
  61.3 0.0 collective-permute-done.2.right_ref
  61.3 2.3 %all-to-all-done.1.self_ref = bf16[16,32,128]{2,1,0:T(8,128)(2,1)S(1)} async-done(((bf16[16,32,128]{2,1,0:T(8,128)(2,1)}), bf16[16,32,128]{2,1,0:T(8,128)(2,1)S(1)}, u32[]{:S(2)}, u32[]{:S(2)}) %all-to-all-start.1) | async-done | bytes 131104 | tf_op jit(solution)/shard_map/all_to_all | solution.py:208
  63.6 0.0 copy-done
  63.6 1.1 %mix.1 = bf16[1,32,2048]{2,1,0:T(8,128)(2,1)} custom-call(s32[1]{0:T(128)} %bitcast.yh_ref.flip_ref, bf16[16,32,128]{2,1,0:T(8,128)(2,1)S(1)} %all-to-all-done.1.self_ref, bf16[32,2048]{1,0:T(8,128)(2,1)S(1)} %bitcast.9, bf16[16,64,128]{2,1,0:T(8,128)(2,1)S(1)} %collective-permute-done.1.left_ref, bf16[16,64,128]{2,1,0:T(8,128)(2,1)S(1)} %collective-permute-done.2.right_ref, ...), custom_call_target="tpu_custom_call" | custom-call | tf_op jit(solution)/shard_map/mix/pallas_call | solution.py:211
Async XLA Ops:
  38.1 11.2 %collective-permute-start = (bf16[32,64,128]{2,1,0:T(8,128)(2,1)S(1)}, bf16[32,64,128]{2,1,0:T(8,128)(2,1)S(1)}, u32[]{:S(2)}, u32[]{:S(2)}) collective-permute-start(bf16[32,64,128]{2,1,0:T(8,128)(2,1)S(1)} %slice.4), channel_id=1, source_target_pairs={{0,1},{1,0},{2,3},{3,2},{4,5},{5,4},{6,7},{7,6},{8,9},{9,8},{10,11... | collective-permute-start | bytes 1572872 | tf_op jit(solution)/shard_map/ppermute | solution.py:190
  41.3 20.0 %collective-permute-start.1 = (bf16[16,64,128]{2,1,0:T(8,128)(2,1)S(1)}, bf16[16,64,128]{2,1,0:T(8,128)(2,1)S(1)}, u32[]{:S(2)}, u32[]{:S(2)}) collective-permute-start(bf16[16,64,128]{2,1,0:T(8,128)(2,1)S(1)} %get-tuple-element.8), channel_id=1, source_target_pairs={{0,64},{64,128},{128,192},{192,256},{256,320},{320,384},{384,448},... | collective-permute-start | bytes 786440 | tf_op jit(solution)/shard_map/ppermute | solution.py:153
  44.4 16.9 %collective-permute-start.2 = (bf16[16,64,128]{2,1,0:T(8,128)(2,1)S(1)}, bf16[16,64,128]{2,1,0:T(8,128)(2,1)S(1)}, u32[]{:S(2)}, u32[]{:S(2)}) collective-permute-start(bf16[16,64,128]{2,1,0:T(8,128)(2,1)S(1)} %get-tuple-element.8), channel_id=1, source_target_pairs={{0,448},{64,0},{128,64},{192,128},{256,192},{320,256},{384,320},{4... | collective-permute-start | bytes 786440 | tf_op jit(solution)/shard_map/ppermute | solution.py:153
  51.4 12.2 %all-to-all-start.1 = ((bf16[16,32,128]{2,1,0:T(8,128)(2,1)}), bf16[16,32,128]{2,1,0:T(8,128)(2,1)S(1)}, u32[]{:S(2)}, u32[]{:S(2)}) async-start(bf16[16,32,128]{2,1,0:T(8,128)(2,1)} %self.1), calls=%async_computation.1 | async-start | bytes 262144 | tf_op jit(solution)/shard_map/all_to_all | solution.py:208
  60.5 3.1 %copy-start = (bf16[1,32,2048]{2,1,0:T(8,128)(2,1)S(1)}, bf16[1,32,2048]{2,1,0:T(8,128)(2,1)}, u32[]{:S(2)}) copy-start(bf16[1,32,2048]{2,1,0:T(8,128)(2,1)} %param.9) | copy-start | bytes 393220

commit v8 on v7

--- a/solution.py
+++ b/solution.py
@@ -125,7 +125,7 @@
             out_ref[seat(IN_Z[line], side ^ IN_YL, yh_ref[0])] = mixed[i * part : (i + 1) * part]
 
 
-def mix_kernel(scale, flip_ref, self_ref, q_ref, left_ref, right_ref, gate_ref, out_ref):
+def cross_kernel(scale, q_ref, left_ref, right_ref, gate_ref, out_ref):
     rows = q_ref.shape[0]
     both = lambda head, part: jnp.concatenate([left_ref[head, part], right_ref[head, part]], axis=0)
     lanes = [slice(head * 128, (head + 1) * 128) for head in range(HEADS)]
@@ -137,14 +137,20 @@
     inverse = 1.0 / jnp.sum(weights, axis=1, keepdims=True)
     weights = weights.astype(jnp.bfloat16)
     for head in range(HEADS):
-        z, yl = divmod(head, 2)
         at = slice(head * rows, (head + 1) * rows)
         numerator = jnp.dot(
             weights[at], both(head, slice(rows, None)), preferred_element_type=jnp.float32
         )
-        cross = numerator * (inverse[at] * gate_ref[1:2, lanes[head]])
-        out_ref[0, :, lanes[head]] = (
-            self_ref[seat(z, yl, flip_ref[0])].astype(jnp.float32) * gate_ref[0:1, lanes[head]] + cross
+        out_ref[:, lanes[head]] = numerator * (inverse[at] * gate_ref[1:2, lanes[head]])
+
+
+def mix_kernel(flip_ref, self_ref, cross_ref, gate_ref, out_ref):
+    for head in range(HEADS):
+        z, yl = divmod(head, 2)
+        lanes = slice(head * 128, (head + 1) * 128)
+        out_ref[0, :, lanes] = (
+            self_ref[seat(z, yl, flip_ref[0])].astype(jnp.float32) * gate_ref[0:1, lanes]
+            + cross_ref[:, lanes]
         ).astype(jnp.bfloat16)
 
 
@@ -187,6 +193,14 @@
         compiler_params=grant(1),
         name="pick",
     )(timestep, pltpu.with_memory_space_constraint(mod_table, pltpu.HBM))
+    cross = pl.pallas_call(
+        functools.partial(cross_kernel, scale),
+        out_shape=jax.ShapeDtypeStruct((rows, width), jnp.float32),
+        in_specs=[VMEM] * 4,
+        out_specs=VMEM,
+        compiler_params=grant(8),
+        name="cross",
+    )(q_cross[0], left, right, gates)
     other = lax.ppermute(mine[:, : 2 * rows], "sp", [(i, i ^ 1) for i in range(64)])
     whole = lambda *shape: pl.BlockSpec(shape, lambda i, yh: (0,) * len(shape))
     part = pl.pallas_call(
@@ -209,13 +223,13 @@
         part, "sp", split_axis=0, concat_axis=0, axis_index_groups=half_owners(), tiled=True
     )
     return pl.pallas_call(
-        functools.partial(mix_kernel, scale),
+        mix_kernel,
         out_shape=jax.ShapeDtypeStruct((1, rows, width), jnp.bfloat16),
-        in_specs=[pl.BlockSpec(memory_space=pltpu.SMEM)] + [VMEM] * 5,
+        in_specs=[pl.BlockSpec(memory_space=pltpu.SMEM)] + [VMEM] * 3,
         out_specs=VMEM,
         compiler_params=grant(8),
         name="mix",
-    )(lower, own, q_cross[0], left, right, gates)
+    )(lower, own, cross, gates)
 
 
 def solution(mesh):

time: 65.2 us -> 64.8 us (level)
  transfers between devices with their start and end apart: 4 -> 4, of which waited for: 1 -> 1; matrix products, arithmetic and copies ran while one was open for 0% -> 0% of each run, Pallas kernels for 4% -> 5%
where the time goes in v8:
time: 64.8 us; the launch traced here: 64.3 us
  blocking collectives  36.8 us (57%)
  starting transfers between devices  19.6 us (30%)
  Pallas kernels  5.19 us (8%)
  waiting for transfers between devices  1.7 us (3%)
  between operations  0.77 us (1%)
    all_to_all x1, blocking collectives, local(): lax.all_to_all(pieces, 'sp', split_axis=0, concat_axis=0, axis_index_grou...  36.8 us
    all_to_all x1, starting transfers between devices, local(): lax.all_to_all(part, 'sp', split_axis=0, concat_axis=0, axis_index_groups...  8.46 us
    ppermute x2, starting transfers between devices, shift(): return lax.ppermute(value, 'cam', pairs)  7.97 us
    ppermute x1, starting transfers between devices, local(): lax.ppermute(mine[:, :2 * rows], 'sp', [(i, i ^ 1) for i in range(64)])  3.19 us
    pallas_call x1, Pallas kernels, local(): pl.pallas_call(functools.partial(self_kernel, scale), out_shape=jax.Shape...  2.09 us
    all_to_all x1, waiting for transfers between devices, local(): lax.all_to_all(part, 'sp', split_axis=0, concat_axis=0, axis_index_groups...  1.69 us
  transfers between devices with their start and end apart: 4, of which 1 were waited for; matrix products, arithmetic and copies ran while one was open for 0% of the time, Pallas kernels for 5%

profile of v8, /device:TPU:1, one launch (start us, length us, event | category | flops | bytes accessed | tf_op | source)
XLA Modules:
  0.0 64.3 jit_solution(3251918374204001569)
XLA Ops:
  0.0 1.2 %pack.1 = (bf16[32,96,128]{2,1,0:T(8,128)(2,1)S(1)}, bf16[16,64,128]{2,1,0:T(8,128)(2,1)S(1)}) custom-call(bf16[32,2048]{1,0:T(8,128)(2,1)} %bitcast.10, bf16[32,2048]{1,0:T(8,128)(2,1)} %bitcast.11, bf16[32,2048]{1,0:T(8,128)(2,1)} %bitcast.12), custom_call_target="tpu_custom_call" | custom-call | tf_op jit(solution)/shard_map/pack/pallas_call | solution.py:167
  1.2 36.8 %all_to_all.10 = bf16[32,96,128]{2,1,0:T(8,128)(2,1)S(1)} all-to-all(bf16[32,96,128]{2,1,0:T(8,128)(2,1)S(1)} %get-tuple-element.7), channel_id=1, replica_groups={{44,46,40,42,4,6,0,2,12,14,8,10,20,22,16,18,28,30,24,26,36,38,32,34,52,..., dimensions={0} | all-to-all | bytes 1572864 | tf_op jit(solution)/shard_map/all_to_all | solution.py:182
  38.0 0.1 slice.4
  38.1 3.2 %collective-permute-start = (bf16[32,64,128]{2,1,0:T(8,128)(2,1)S(1)}, bf16[32,64,128]{2,1,0:T(8,128)(2,1)S(1)}, u32[]{:S(2)}, u32[]{:S(2)}) collective-permute-start(bf16[32,64,128]{2,1,0:T(8,128)(2,1)S(1)} %slice.4), channel_id=1, source_target_pairs={{0,1},{1,0},{2,3},{3,2},{4,5},{5,4},{6,7},{7,6},{8,9},{9,8},{10,11... | collective-permute-start | bytes 1572872 | tf_op jit(solution)/shard_map/ppermute | solution.py:204
  41.3 3.1 %collective-permute-start.1 = (bf16[16,64,128]{2,1,0:T(8,128)(2,1)S(1)}, bf16[16,64,128]{2,1,0:T(8,128)(2,1)S(1)}, u32[]{:S(2)}, u32[]{:S(2)}) collective-permute-start(bf16[16,64,128]{2,1,0:T(8,128)(2,1)S(1)} %get-tuple-element.8), channel_id=1, source_target_pairs={{0,64},{64,128},{128,192},{192,256},{256,320},{320,384},{384,448},... | collective-permute-start | bytes 786440 | tf_op jit(solution)/shard_map/ppermute | solution.py:159
  44.4 4.8 %collective-permute-start.2 = (bf16[16,64,128]{2,1,0:T(8,128)(2,1)S(1)}, bf16[16,64,128]{2,1,0:T(8,128)(2,1)S(1)}, u32[]{:S(2)}, u32[]{:S(2)}) collective-permute-start(bf16[16,64,128]{2,1,0:T(8,128)(2,1)S(1)} %get-tuple-element.8), channel_id=1, source_target_pairs={{0,448},{64,0},{128,64},{192,128},{256,192},{320,256},{384,320},{4... | collective-permute-start | bytes 786440 | tf_op jit(solution)/shard_map/ppermute | solution.py:159
  49.3 0.0 collective-permute-done
  49.3 2.1 %self.1 = bf16[16,32,128]{2,1,0:T(8,128)(2,1)} custom-call(s32[1]{0:T(128)} %bitcast.yh_ref.flip_ref, bf16[8,2,2,96,128]{4,3,2,1,0:T(8,128)(2,1)S(1)} %bitcast.7, bf16[8,2,2,64,128]{4,3,2,1,0:T(8,128)(2,1)S(1)} %bitcast.8), custom_call_target="tpu_custom_call" | custom-call | tf_op jit(solution)/shard_map/self/pallas_call | solution.py:206
  51.4 8.5 %all-to-all-start.1 = ((bf16[16,32,128]{2,1,0:T(8,128)(2,1)}), bf16[16,32,128]{2,1,0:T(8,128)(2,1)S(1)}, u32[]{:S(2)}, u32[]{:S(2)}) async-start(bf16[16,32,128]{2,1,0:T(8,128)(2,1)} %self.1), calls=%async_computation.1 | async-start | bytes 262144 | tf_op jit(solution)/shard_map/all_to_all | solution.py:222
  60.5 0.0 copy-start
  60.5 0.8 %pick.1.gate_ref = f32[2,2048]{1,0:T(2,128)S(1)} custom-call(s32[1]{0:T(128)S(6)} %copy.7.step_ref, f32[50,2,2048]{2,1,0:T(2,128)} %table_ref.1), custom_call_target="tpu_custom_call" | custom-call | tf_op jit(solution)/shard_map/pick/pallas_call | solution.py:187
  61.3 0.0 collective-permute-done.1.left_ref
  61.3 0.0 collective-permute-done.2.right_ref
  61.3 0.1 copy-done
  61.4 0.5 cross.1.cross_ref
  61.9 1.7 %all-to-all-done.1.self_ref = bf16[16,32,128]{2,1,0:T(8,128)(2,1)S(1)} async-done(((bf16[16,32,128]{2,1,0:T(8,128)(2,1)}), bf16[16,32,128]{2,1,0:T(8,128)(2,1)S(1)}, u32[]{:S(2)}, u32[]{:S(2)}) %all-to-all-start.1) | async-done | bytes 131104 | tf_op jit(solution)/shard_map/all_to_all | solution.py:222
  63.6 0.7 %mix.1 = bf16[1,32,2048]{2,1,0:T(8,128)(2,1)} custom-call(s32[1]{0:T(128)} %bitcast.yh_ref.flip_ref, bf16[16,32,128]{2,1,0:T(8,128)(2,1)S(1)} %all-to-all-done.1.self_ref, f32[32,2048]{1,0:T(8,128)S(1)} %cross.1.cross_ref, f32[2,2048]{1,0:T(2,128)S(1)} %pick.1.gate_ref), custom_call_target="tpu_custom_call" | custom-call | tf_op jit(solution)/shard_map/mix/pallas_call | solution.py:225
Async XLA Ops:
  38.1 11.2 %collective-permute-start = (bf16[32,64,128]{2,1,0:T(8,128)(2,1)S(1)}, bf16[32,64,128]{2,1,0:T(8,128)(2,1)S(1)}, u32[]{:S(2)}, u32[]{:S(2)}) collective-permute-start(bf16[32,64,128]{2,1,0:T(8,128)(2,1)S(1)} %slice.4), channel_id=1, source_target_pairs={{0,1},{1,0},{2,3},{3,2},{4,5},{5,4},{6,7},{7,6},{8,9},{9,8},{10,11... | collective-permute-start | bytes 1572872 | tf_op jit(solution)/shard_map/ppermute | solution.py:204
  41.3 20.0 %collective-permute-start.1 = (bf16[16,64,128]{2,1,0:T(8,128)(2,1)S(1)}, bf16[16,64,128]{2,1,0:T(8,128)(2,1)S(1)}, u32[]{:S(2)}, u32[]{:S(2)}) collective-permute-start(bf16[16,64,128]{2,1,0:T(8,128)(2,1)S(1)} %get-tuple-element.8), channel_id=1, source_target_pairs={{0,64},{64,128},{128,192},{192,256},{256,320},{320,384},{384,448},... | collective-permute-start | bytes 786440 | tf_op jit(solution)/shard_map/ppermute | solution.py:159
  44.4 16.9 %collective-permute-start.2 = (bf16[16,64,128]{2,1,0:T(8,128)(2,1)S(1)}, bf16[16,64,128]{2,1,0:T(8,128)(2,1)S(1)}, u32[]{:S(2)}, u32[]{:S(2)}) collective-permute-start(bf16[16,64,128]{2,1,0:T(8,128)(2,1)S(1)} %get-tuple-element.8), channel_id=1, source_target_pairs={{0,448},{64,0},{128,64},{192,128},{256,192},{320,256},{384,320},{4... | collective-permute-start | bytes 786440 | tf_op jit(solution)/shard_map/ppermute | solution.py:159
  51.4 12.2 %all-to-all-start.1 = ((bf16[16,32,128]{2,1,0:T(8,128)(2,1)}), bf16[16,32,128]{2,1,0:T(8,128)(2,1)S(1)}, u32[]{:S(2)}, u32[]{:S(2)}) async-start(bf16[16,32,128]{2,1,0:T(8,128)(2,1)} %self.1), calls=%async_computation.1 | async-start | bytes 262144 | tf_op jit(solution)/shard_map/all_to_all | solution.py:222
  60.5 0.9 %copy-start = (bf16[1,32,2048]{2,1,0:T(8,128)(2,1)S(1)}, bf16[1,32,2048]{2,1,0:T(8,128)(2,1)}, u32[]{:S(2)}) copy-start(bf16[1,32,2048]{2,1,0:T(8,128)(2,1)} %param.9) | copy-start | bytes 393220
